TPU v7x, 128 devices: a whole 4x4x4 slice. The times are simulated.
128 devices in a mesh: ctx: 16 (over z, y), ch: 8 (over x, core).
Axes of the slice: x: 4, y: 4, z: 4, core: 2. Of those that a mesh axis runs over, the one named last changes fastest.
Arguments:
- outer_gate: bfloat16 [4096, 4096], P('ctx', 'ch'), may hold values from -6 to 6
- inner_gate: bfloat16 [4096, 4096], P('ctx', 'ch'), may hold values from -6 to 6
- values_in: bfloat16 [4096, 4096], P('ctx', 'ch'), may hold values from -6 to 6
- filters: float32 [4096, 4096], P('ctx', 'ch'), as said below
- skip_gain: float32 [4096], P('ch'), may hold values from 0.5 to 1.5
- w_out: bfloat16 [4096, 4096], P('ch', 'ctx'), may hold values from -0.125 to 0.125
Outputs:
- mixed: bfloat16 [4096, 4096], P('ctx', 'ch')
Inputs may be any that keep to these rules, and one draw needn't show every extreme that they name: `filters`: finite values.
All inputs are finite; a program needn't handle non-finite values.
Results may differ from a plain program's by a relative error of at most 0.022.
Values may be sent and summed in bfloat16 or wider, within the bound.
A program may use at most 64 MiB of HBM per device.

v0:
```python
import math

import jax
import jax.numpy as jnp
from jax import lax
from jax.sharding import PartitionSpec as P


def from_behind(block, axis, distance):
    devices = range(lax.axis_size(axis))
    route = [(i - distance, i) for i in devices if i - distance in devices]
    return lax.ppermute(block, axis, route)


def forward_table(block):
    length = 2 * block
    rows = jnp.arange(block, dtype=jnp.int32)[:, None]
    freqs = jnp.arange(length, dtype=jnp.int32)[None, :]
    angles = 2.0 * math.pi / length * (rows * freqs % length).astype(jnp.float32)
    return jnp.concatenate([jnp.cos(angles), -jnp.sin(angles)], axis=1)


def inverse_table(block):
    length = 2 * block
    freqs = jnp.arange(length, dtype=jnp.int32)[:, None]
    places = jnp.arange(length, dtype=jnp.int32)[None, :]
    angles = 2.0 * math.pi / length * (freqs * places % length).astype(jnp.float32)
    return jnp.concatenate([jnp.cos(angles), -jnp.sin(angles)], axis=0) / length


def split_table(table):
    upper_part = table.astype(jnp.bfloat16)
    lower_part = (table - upper_part.astype(jnp.float32)).astype(jnp.bfloat16)
    return (upper_part, lower_part)


def spectrum(series, table):
    return lax.dot_general(
        series,
        table,
        (((0,), (0,)), ((), ())),
        precision=lax.Precision.HIGH,
        preferred_element_type=jnp.float32,
    )


def narrow_spectrum(series, tables):
    dims = (((0,), (0,)), ((), ()))
    first = lax.dot_general(series, tables[0], dims, preferred_element_type=jnp.float32)
    return first + lax.dot_general(series, tables[1], dims, preferred_element_type=jnp.float32)


def complex_product(left, right):
    half = left.shape[-1] // 2
    left_re, left_im = (left[..., :half], left[..., half:])
    right_re, right_im = (right[..., :half], right[..., half:])
    return jnp.concatenate(
        [left_re * right_re - left_im * right_im, left_re * right_im + left_im * right_re], axis=-1
    )


def per_device(outer_gate, inner_gate, values_in, filters, skip_gain, w_out):
    block = outer_gate.shape[0]
    chans = outer_gate.shape[1]
    length = 2 * block
    gated = (inner_gate.astype(jnp.float32) * values_in.astype(jnp.float32)).astype(jnp.bfloat16)
    forward = forward_table(block)
    forward_parts = split_table(forward)
    inverse = inverse_table(block)
    whole_filter = lax.all_gather(filters.astype(jnp.bfloat16), "ctx", axis=0, tiled=True).astype(
        filters.dtype
    )
    mine = lax.axis_index("ctx")
    empty = jnp.zeros((chans, 2 * length), jnp.float32)
    piece = lax.all_gather(gated[None], "ctx", axis=0, tiled=True)

    def one_block(k, acc):
        distance = mine - k

        def live(inner):
            lag_rows = lax.dynamic_slice_in_dim(
                whole_filter, jnp.maximum(distance, 0) * block, block, 0
            )
            source = lax.dynamic_index_in_dim(piece, k, 0, keepdims=False)
            return inner + complex_product(
                narrow_spectrum(source, forward_parts), spectrum(lag_rows, forward)
            )

        return lax.cond(distance >= 0, live, lambda inner: inner, acc)

    summed = lax.fori_loop(0, piece.shape[0], one_block, empty)
    wave = lax.dot_general(
        inverse,
        summed,
        (((0,), (1,)), ((), ())),
        precision=lax.Precision.HIGH,
        preferred_element_type=jnp.float32,
    )
    carried = from_behind(wave[block:].astype(jnp.bfloat16), "ctx", 1).astype(jnp.float32)
    conv = wave[:block] + carried
    mix_in = (
        outer_gate.astype(jnp.float32) * (conv + skip_gain[None, :] * gated.astype(jnp.float32))
    ).astype(jnp.bfloat16)
    partial_rows = jnp.dot(
        mix_in, lax.all_gather(w_out, "ctx", axis=1, tiled=True), preferred_element_type=jnp.float32
    )
    return lax.psum_scatter(
        partial_rows.astype(jnp.bfloat16), "ch", scatter_dimension=1, tiled=True
    )


def solution(mesh):
    placed = (
        P("ctx", "ch"),
        P("ctx", "ch"),
        P("ctx", "ch"),
        P("ctx", "ch"),
        P("ch"),
        P("ch", "ctx"),
    )
    return jax.shard_map(
        per_device, mesh=mesh, in_specs=placed, out_specs=P("ctx", "ch"), check_vma=False
    )
```

profile of v0, /device:TPU:1, one launch (start us, length us, event | category | flops | bytes accessed | tf_op | source)
XLA Modules:
  0.0 320.2 jit_solution(1819847222807152443)
XLA Ops:
  6.5 0.0 all-gather.5.cloned.1.call-start
  6.5 1.8 convert_element_type.66
  8.3 0.0 all-gather.5.cloned.1.call-update
  8.3 0.0 all-gather.9.cloned.1.call-start
  8.4 1.8 multiply_convert_fusion
  10.2 0.0 all-gather.9.cloned.1.call-update
  10.2 0.0 all-gather.7.cloned.1.call-start
  10.3 0.7 all-gather.7.cloned.1.call-update
  10.9 0.0 reduce-scatter.2.cloned.1.call-start
  11.0 2.1 sine_negate_fusion.1
  13.1 0.9 fusion.35
  13.9 1.0 pad_maximum_fusion
  14.9 5.0 %sine_negate_fusion = (f32[512,512]{1,0:T(8,128)}, f32[512,512]{1,0:T(8,128)}) fusion(), kind=kLoop, calls=%fused_computation.28 | loop fusion | flops 3932160 | bytes 2097152 | tf_op jit(solution)/shard_map/neg | solution.py:28
  19.9 44.5 %all-gather.5.cloned.1.call-done = bf16[4096,512]{1,0:T(8,128)(2,1)} async-done(((bf16[256,512]{1,0:T(8,128)(2,1)}), bf16[4096,512]{1,0:T(8,128)(2,1)}) %all-gather.5.cloned.1.call-update) | async-done | bytes 4194320 | tf_op jit(solution)/shard_map/all_gather | solution.py:70
  64.4 6.6 %convert_element_type.67 = f32[4096,512]{1,0:T(8,128)} convert(bf16[4096,512]{1,0:T(8,128)(2,1)} %all-gather.5.cloned.1.call-done) | non-fusion elementwise | flops 2097152 | bytes 12582912 | tf_op jit(solution)/shard_map/convert_element_type | solution.py:70
  71.0 46.8 %all-gather.9.cloned.1.call-done = bf16[4096,512]{1,0:T(8,128)(2,1)} async-done(((bf16[256,512]{1,0:T(8,128)(2,1)}), bf16[4096,512]{1,0:T(8,128)(2,1)}) %all-gather.9.cloned.1.call-update) | async-done | bytes 4194320 | tf_op jit(solution)/shard_map/all_gather | solution.py:75
  117.8 1.6 broadcast_in_dim.4
  119.4 9.3 %while.16 = (s32[]{:T(128)}, f32[512,1024]{1,0:T(8,128)}, s32[]{:T(128)}, bf16[16,256,512]{2,1,0:T(8,128)(2,1)}, bf16[256,1024]{1,0:T(8,128)(2,1)}, /*index=5*/b...) while((s32[]{:T(128)}, f32[512,1024]{1,0:T(8,128)}, ...), condition=%wide.region_3.4_spmd, body=%wide.region_0.3_spmd.sunk | while | flops 1345323008 | bytes 26214732 | solution.py:91
  119.4 9.0 %conditional.2 = (f32[512,1024]{1,0:T(8,128)}) conditional(s32[]{:T(128)} %convert_element_type.104, f32[512,1024]{1,0:T(8,128)} %get-tuple-element.261, (s32[]{:T(128)}, bf16[16,256,512]{2,1,0:T(8,128)(2,1)}, bf16[256,1024]{1,0:T(8,128)(2,1)}, bf16[256,1024]{1,0:T(8,128)(2,1)}, s32[]{:T(128)}, /*index=5*/f32[4096,512]{1,0:T(8,128)}, ...), branch_computations={%region_1.1_spmd, %region_2.2_spmd} | conditional | flops 1345323008 | bytes 26214540 | solution.py:89
  119.4 0.0 copy-start
  119.4 1.6 fusion.3
  121.1 0.0 copy-done
  121.1 1.4 convolution_add_fusion
  122.5 2.1 fusion
  124.6 0.5 multiply_subtract_fusion
  125.1 3.3 %maximum_add_fusion = f32[512,1024]{1,0:T(8,128)} fusion(f32[512,1024]{1,0:T(8,128)} %get-tuple-element.158, f32[512,512]{1,0:T(8,128)S(1)} %get-tuple-element.194, f32[512,512]{1,0:T(8,128)S(1)} %get-tuple-element.193), kind=kLoop, calls=%fused_computation | loop fusion | flops 1048576 | bytes 6291456 | tf_op jit(solution)/shard_map/while/body/eval_jaxpr/cond/branch_1_fun/add | solution.py:85
  128.8 0.0 copy-start.1
  128.8 0.0 copy-start.2
  128.8 0.0 copy-start.3
  128.8 5.9 %fusion.10 = f32[512,512]{1,0:T(8,128)S(1)} fusion(f32[512,1024]{1,0:T(8,128)} %get-tuple-element.176, f32[512,512]{1,0:T(8,128)} %get-tuple-element.199, f32[512,512]{1,0:T(8,128)} %get-tuple-element.200), kind=kOutput, calls=%fused_computation.16 | convolution fusion | flops 1611661312 | bytes 5242880 | tf_op jit(solution)/shard_map/dot_general | solution.py:92
  134.7 12.1 %collective-permute-start = (bf16[256,512]{1,0:T(8,128)(2,1)S(1)}, bf16[256,512]{1,0:T(8,128)(2,1)S(1)}, u32[]{:S(2)}, u32[]{:S(2)}) collective-permute-start(bf16[256,512]{1,0:T(8,128)(2,1)S(1)} %slice.44), channel_id=1, source_target_pairs={{0,8},{8,16},{16,24},{24,32},{32,40},{40,48},{48,56},{56,64},{64,7... | collective-permute-start | bytes 786440 | tf_op jit(solution)/shard_map/ppermute | solution.py:12
  146.8 29.3 %all-gather.7.cloned.1.call-done = bf16[512,4096]{1,0:T(8,128)(2,1)} async-done(((bf16[512,256]{1,0:T(8,128)(2,1)}), bf16[512,4096]{1,0:T(8,128)(2,1)}) %all-gather.7.cloned.1.call-update) | async-done | bytes 4194320 | tf_op jit(solution)/shard_map/all_gather | solution.py:105
  176.1 0.0 collective-permute-done
  176.1 0.0 copy-done.1
  176.1 0.0 copy-done.2
  176.1 0.0 copy-done.3
  176.1 4.8 %convolution_convert_fusion = bf16[256,4096]{1,0:T(8,128)(2,1)} fusion(bf16[512,4096]{1,0:T(8,128)(2,1)} %all-gather.7.cloned.1.call-done, f32[512,512]{1,0:T(8,128)S(1)} %fusion.10, bf16[256,512]{1,0:T(8,128)(2,1)S(1)} %copy-done.1, bf16[256,512]{1,0:T(8,128)(2,1)S(1)} %collective-permute-done, bf16[256,512]{1,0:T(8,128)(2,1)S(1)} %copy-done.2, ...), kind=kOutput, calls=%fused_computation.14 | convolution fusion | flops 1075838976 | bytes 7604224 | tf_op jit(solution)/shard_map/dot_general | solution.py:104
  180.9 0.0 reduce-scatter.2.cloned.1.call-update
  180.9 132.8 %reduce-scatter.2.cloned.1.call-done = bf16[256,512]{1,0:T(8,128)(2,1)} async-done(((bf16[256,4096]{1,0:T(8,128)(2,1)}), bf16[256,512]{1,0:T(8,128)(2,1)}) %reduce-scatter.2.cloned.1.call-update) | async-done | bytes 262160 | tf_op jit(solution)/shard_map/reduce_scatter | solution.py:107
  (16 shorter events, 0.1 us)
Async XLA Ops:
  6.5 57.9 %all-gather.5.cloned.1.call-start = ((), (), s32[]{:S(2)}) async-start(), calls=%async_computation.1 | async-start | bytes 4456448 | tf_op jit(solution)/shard_map/all_gather | solution.py:70
  8.3 109.5 %all-gather.9.cloned.1.call-start = ((), (), s32[]{:S(2)}) async-start(), calls=%async_computation.4 | async-start | bytes 4456448 | tf_op jit(solution)/shard_map/all_gather | solution.py:75
  10.2 165.9 %all-gather.7.cloned.1.call-start = ((), (), s32[]{:S(2)}) async-start(), calls=%async_computation.2 | async-start | bytes 4456448 | tf_op jit(solution)/shard_map/all_gather | solution.py:105
  10.9 302.8 %reduce-scatter.2.cloned.1.call-start = ((), (), s32[]{:S(2)}) async-start(), calls=%async_computation.3 | async-start | bytes 2359296 | tf_op jit(solution)/shard_map/reduce_scatter | solution.py:107
  119.4 1.6 copy-start
  128.8 47.3 %copy-start.1 = (bf16[256,512]{1,0:T(8,128)(2,1)S(1)}, bf16[256,512]{1,0:T(8,128)(2,1)}, u32[]{:S(2)}) copy-start(bf16[256,512]{1,0:T(8,128)(2,1)} %multiply_convert_fusion) | copy-start | bytes 786436
  128.8 47.3 %copy-start.2 = (bf16[256,512]{1,0:T(8,128)(2,1)S(1)}, bf16[256,512]{1,0:T(8,128)(2,1)}, u32[]{:S(2)}) copy-start(bf16[256,512]{1,0:T(8,128)(2,1)} %param.10) | copy-start | bytes 786436
  128.8 47.3 %copy-start.3 = (f32[512]{0:T(512)S(1)}, f32[512]{0:T(512)}, u32[]{:S(2)}) copy-start(f32[512]{0:T(512)} %param.14) | copy-start | bytes 6148
  134.7 41.3 %collective-permute-start = (bf16[256,512]{1,0:T(8,128)(2,1)S(1)}, bf16[256,512]{1,0:T(8,128)(2,1)S(1)}, u32[]{:S(2)}, u32[]{:S(2)}) collective-permute-start(bf16[256,512]{1,0:T(8,128)(2,1)S(1)} %slice.44), channel_id=1, source_target_pairs={{0,8},{8,16},{16,24},{24,32},{32,40},{40,48},{48,56},{56,64},{64,7... | collective-permute-start | bytes 786440 | tf_op jit(solution)/shard_map/ppermute | solution.py:12
Sparse Core Ops, SparseCore 0:
  9.5 54.8 all-gather.4
  66.5 51.2 all-gather.8
  119.9 56.0 all-gather.6
  181.0 132.6 reduce-scatter.1
where the time goes:
time: 325 us; the launch traced here: 320 us
  waiting for transfers between devices  254 us (78%)
  other arithmetic  22.9 us (7%)
  matrix products  15.8 us (5%)
  between operations  13.2 us (4%)
  starting transfers between devices  12.2 us (4%)
    reduce_scatter x1, waiting for transfers between devices, per_device(): lax.psum_scatter(partial_rows.astype(jnp.bfloat16), 'ch', scatter_dimensi...  133 us
    all_gather x1, waiting for transfers between devices, per_device(): piece = lax.all_gather(gated[None], 'ctx', axis=0, tiled=True)  46.8 us
    all_gather x1, waiting for transfers between devices, per_device(): lax.all_gather(filters.astype(jnp.bfloat16), 'ctx', axis=0, tiled=True)  44.5 us
    all_gather x1, waiting for transfers between devices, per_device(): lax.all_gather(w_out, 'ctx', axis=1, tiled=True)  29.3 us
    ppermute x1, starting transfers between devices, from_behind(): return lax.ppermute(block, axis, route)  12.1 us
    convert_element_type x1, other arithmetic, per_device(): lax.all_gather(filters.astype(jnp.bfloat16), 'ctx', axis=0, tiled=True)  6.63 us
  transfers between devices with their start and end apart: 5, of which 4 were waited for; matrix products, arithmetic and copies ran while one was open for 11% of the time, Pallas kernels for 0%

commit v1 on v0

v1 whole, which is shorter than its diff:
```python
import functools

import jax
import jax.numpy as jnp
import numpy as np
from jax import lax
from jax.experimental import pallas as pl
from jax.experimental.pallas import tpu as pltpu
from jax.sharding import PartitionSpec as P

BF16 = jnp.bfloat16
F32 = jnp.float32
RING = 4


def forward_table(block):
    place = np.arange(block, dtype=np.int64)[:, None]
    freq = np.arange(block, dtype=np.int64)[None, :]
    angle = np.pi / (2 * block) * (place * (2 * freq + 1) % (4 * block)).astype(np.float64)
    return np.concatenate([np.cos(angle), -np.sin(angle)], axis=1).astype(jnp.bfloat16)


def inverse_table(block):
    freq = np.arange(block, dtype=np.int64)[:, None]
    place = np.arange(2 * block, dtype=np.int64)[None, :]
    angle = np.pi / (2 * block) * (place * (2 * freq + 1) % (4 * block)).astype(np.float64)
    return (np.concatenate([np.cos(angle), -np.sin(angle)], axis=0) / block).astype(jnp.bfloat16)


def kernel(
    og_h, ig_h, vi_h, fl_h, sk_ref, w_h, ft_h, it_h, out_ref,
    og, ig, vi, fl, ft, it, gated, gsend, hsend, gx, hx, gs, hs, ys, ps, csend, cx, mix, wall,
    part, other, cr, s1, r1, s2, r2,
    ld, gsem_s, gsem_r, hsem_s, hsem_r, csem_s, csem_r, wsem_s, wsem_r, osem_s, osem_r, xsem_s, xsem_r,
):
    nctx = 16
    me = lax.axis_index("ctx")
    mych = lax.axis_index("ch")
    y, z = lax.rem(me, RING), me // RING
    x, core = mych // 2, lax.rem(mych, 2)
    sub = gsend.shape[0] // nctx
    half = w_h.shape[0] // 2

    def ctx_of(ry, rz):
        return lax.rem(z + rz + RING, RING) * RING + lax.rem(y + ry + RING, RING)

    def ch_of(rx, c):
        return lax.rem(x + rx + RING, RING) * 2 + c

    loads = [
        pltpu.make_async_copy(src, dst, ld.at[n])
        for n, (src, dst) in enumerate(
            [(ig_h, ig), (vi_h, vi), (fl_h, fl), (w_h, wall.at[me]), (ft_h, ft), (it_h, it), (og_h, og)]
        )
    ]
    for copy in loads:
        copy.start()

    barrier = pltpu.get_barrier_semaphore()
    for d in range(1, nctx):
        pl.semaphore_signal(barrier, inc=1, device_id={"ctx": lax.rem(me + d, nctx)})
    pl.semaphore_signal(barrier, inc=1, device_id={"ch": ch_of(0, 1 - core)})
    pl.semaphore_signal(barrier, inc=1, device_id={"ch": ch_of(1, core)})
    pl.semaphore_signal(barrier, inc=1, device_id={"ch": ch_of(-1, core)})

    sent = []
    kinds = {}

    def w_copy(h, stage, ra, what):
        key = (h, stage, ra, what)
        if key not in kinds:
            kinds[key] = len(kinds)
        n = kinds[key]
        step = 1 if what in ("R", "FR") else -1
        rel = {"R": 0, "L": 0, "FR": -1, "FL": 1}[what]
        rows = {"R": (0, half), "L": (0, half), "FR": (0, half // 2), "FL": (half // 2, half // 2)}[what]
        first, second = (rel, 0) if stage == 0 else (ra, rel)
        chunk = ctx_of(first, second) if h == 0 else ctx_of(second, first)
        along_y = (h == 0) == (stage == 0)
        to = ctx_of(step, 0) if along_y else ctx_of(0, step)
        ref = wall.at[chunk, pl.ds(h * half + rows[0], rows[1])]
        return pltpu.make_async_remote_copy(
            src_ref=ref, dst_ref=ref, send_sem=wsem_s.at[n], recv_sem=wsem_r.at[n], device_id={"ctx": to}
        )

    def w_wait(h, stage, ra, what):
        n = kinds[(h, stage, ra, what)]
        step = 1 if what in ("R", "FR") else -1
        rel = {"R": 0, "L": 0, "FR": -1, "FL": 1}[what] - step
        rows = {"R": (0, half), "L": (0, half), "FR": (0, half // 2), "FL": (half // 2, half // 2)}[what]
        first, second = (rel, 0) if stage == 0 else (ra, rel)
        chunk = ctx_of(first, second) if h == 0 else ctx_of(second, first)
        along_y = (h == 0) == (stage == 0)
        to = ctx_of(step, 0) if along_y else ctx_of(0, step)
        ref = wall.at[chunk, pl.ds(h * half + rows[0], rows[1])]
        pltpu.make_async_remote_copy(
            src_ref=ref, dst_ref=ref, send_sem=wsem_s.at[n], recv_sem=wsem_r.at[n], device_id={"ctx": to}
        ).wait_recv()

    def w_send(h, stage, ra, what):
        copy = w_copy(h, stage, ra, what)
        copy.start()
        sent.append(copy)

    def exchange(src, dst, ssem, rsem, d):
        to = lax.rem(me + d, nctx)
        return pltpu.make_async_remote_copy(
            src_ref=src.at[pl.ds(pl.multiple_of(to * sub, sub), sub)],
            dst_ref=dst.at[pl.ds(pl.multiple_of(me * sub, sub), sub)],
            send_sem=ssem.at[d],
            recv_sem=rsem.at[d],
            device_id={"ctx": to},
        )

    def exchange_wait(src, dst, ssem, rsem, d):
        frm = lax.rem(me - d + nctx, nctx)
        pltpu.make_async_remote_copy(
            src_ref=src.at[pl.ds(pl.multiple_of(frm * sub, sub), sub)],
            dst_ref=dst.at[pl.ds(pl.multiple_of(frm * sub, sub), sub)],
            send_sem=ssem.at[d],
            recv_sem=rsem.at[d],
            device_id={"ctx": frm},
        ).wait_recv()

    def exchange_all(src, dst, ssem, rsem):
        for d in range(1, nctx):
            copy = exchange(src, dst, ssem, rsem, d)
            copy.start()
            sent.append(copy)
        mine = pl.ds(pl.multiple_of(me * sub, sub), sub)
        dst[mine, :] = src[mine, :]

    loads[0].wait()
    loads[1].wait()
    product = (ig[...].astype(F32) * vi[...].astype(F32)).astype(BF16)
    gated[...] = product
    gsend[...] = jnp.transpose(product.astype(F32)).astype(BF16)
    loads[3].wait()
    pl.semaphore_wait(barrier, nctx + 2)
    exchange_all(gsend, gx, gsem_s, gsem_r)
    loads[2].wait()
    hsend[...] = jnp.transpose(fl[...]).astype(BF16)
    exchange_all(hsend, hx, hsem_s, hsem_r)
    for h in (0, 1):
        for what in ("R", "L"):
            w_send(h, 0, 0, what)
    for h in (0, 1):
        for what in ("R", "L"):
            w_send(h, 1, 0, what)

    loads[4].wait()
    for d in range(1, nctx):
        exchange_wait(gsend, gx, gsem_s, gsem_r, d)
    gs[...] = jnp.dot(gx[...], ft[...], preferred_element_type=F32)
    for d in range(1, nctx):
        exchange_wait(hsend, hx, hsem_s, hsem_r, d)
    hs[...] = jnp.dot(hx[...], ft[...], preferred_element_type=F32)

    for h in (0, 1):
        w_wait(h, 0, 0, "R")
        w_send(h, 0, 0, "FR")
        w_send(h, 1, -1, "R")
        w_send(h, 1, -1, "L")
        w_wait(h, 0, 0, "L")
        w_send(h, 0, 0, "FL")
        w_send(h, 1, 1, "R")
        w_send(h, 1, 1, "L")

    bins = gs.shape[1] // 2

    def block_products(n, carry):
        row = pl.multiple_of(n * 8, 8)
        for lane in range(0, bins, 128):
            gr = [gs[pl.ds(b * sub + row, 8), pl.ds(lane, 128)] for b in range(nctx)]
            gi = [gs[pl.ds(b * sub + row, 8), pl.ds(bins + lane, 128)] for b in range(nctx)]
            hr = [hs[pl.ds(b * sub + row, 8), pl.ds(lane, 128)] for b in range(nctx)]
            hi = [hs[pl.ds(b * sub + row, 8), pl.ds(bins + lane, 128)] for b in range(nctx)]
            for i in range(nctx):
                re = gr[0] * hr[i] - gi[0] * hi[i]
                im = gr[0] * hi[i] + gi[0] * hr[i]
                for j in range(1, i + 1):
                    re += gr[j] * hr[i - j] - gi[j] * hi[i - j]
                    im += gr[j] * hi[i - j] + gi[j] * hr[i - j]
                ys[pl.ds(i * sub + row, 8), pl.ds(lane, 128)] = re
                ys[pl.ds(i * sub + row, 8), pl.ds(bins + lane, 128)] = im
        return carry

    lax.fori_loop(0, sub // 8, block_products, 0)

    loads[5].wait()
    ps[...] = jnp.dot(ys[...].astype(BF16), it[...], preferred_element_type=F32)
    csend[pl.ds(0, sub), :] = ps[pl.ds(0, sub), pl.ds(0, bins)].astype(BF16)
    rest = sub * (nctx - 1)
    csend[pl.ds(sub, rest), :] = (
        ps[pl.ds(sub, rest), pl.ds(0, bins)] + ps[pl.ds(0, rest), pl.ds(bins, bins)]
    ).astype(BF16)
    exchange_all(csend, cx, csem_s, csem_r)

    for h in (0, 1):
        w_wait(h, 0, 0, "FR")
        w_wait(h, 0, 0, "FL")
        w_send(h, 1, 2, "R")
        w_send(h, 1, 2, "L")
    for ra in (0, -1, 1):
        for h in (0, 1):
            w_wait(h, 1, ra, "R")
            w_send(h, 1, ra, "FR")
            w_wait(h, 1, ra, "L")
            w_send(h, 1, ra, "FL")

    loads[6].wait()
    for d in range(1, nctx):
        exchange_wait(csend, cx, csem_s, csem_r, d)
    conv = jnp.transpose(cx[...].astype(F32))
    mix[...] = (og[...].astype(F32) * (conv + sk_ref[...] * gated[...].astype(F32))).astype(BF16)

    for ra in (2,):
        for h in (0, 1):
            w_wait(h, 1, ra, "R")
            w_send(h, 1, ra, "FR")
            w_wait(h, 1, ra, "L")
            w_send(h, 1, ra, "FL")
    for ra in (0, -1, 1, 2):
        for h in (0, 1):
            w_wait(h, 1, ra, "FR")
            w_wait(h, 1, ra, "FL")

    cols = w_h.shape[1]

    def columns(rx, c, n):
        q = lax.rem(x + rx + RING, RING)
        return jnp.dot(mix[...], wall[q * RING + c * 2 + n], preferred_element_type=F32)

    turns = (2, 1, -1, 0)
    swaps = []
    for k, rx in enumerate(turns):
        for n in (0, 1):
            other[k, :, n * cols : (n + 1) * cols] = columns(rx, 1 - core, n).astype(BF16)
        copy = pltpu.make_async_remote_copy(
            src_ref=other.at[k], dst_ref=cr.at[k], send_sem=osem_s.at[k], recv_sem=osem_r.at[k],
            device_id={"ch": ch_of(0, 1 - core)},
        )
        copy.start()
        swaps.append(copy)
    for k, rx in enumerate(turns):
        for n in (0, 1):
            part[k, :, n * cols : (n + 1) * cols] = columns(rx, core, n)

    rows = mix.shape[0]
    top, low = pl.ds(0, rows // 2), pl.ds(rows // 2, rows // 2)

    def ring(n, src, dst, step):
        copy = pltpu.make_async_remote_copy(
            src_ref=src, dst_ref=dst, send_sem=xsem_s.at[n], recv_sem=xsem_r.at[n],
            device_id={"ch": ch_of(step, core)},
        )
        copy.start()
        return copy

    swaps[0].wait_recv()
    s1[...] = (part[0] + cr[0].astype(F32)).astype(BF16)
    up1 = ring(0, s1.at[top], r1.at[top], 1)
    down1 = ring(1, s1.at[low], r1.at[low], -1)
    swaps[1].wait_recv()
    s2[0, low, :] = (part[1, low, :] + cr[1, low, :].astype(F32)).astype(BF16)
    up2 = ring(2, s2.at[0, low], r2.at[0, low], 1)
    swaps[2].wait_recv()
    s2[1, top, :] = (part[2, top, :] + cr[2, top, :].astype(F32)).astype(BF16)
    down2 = ring(3, s2.at[1, top], r2.at[1, top], -1)
    up1.wait_recv()
    s2[0, top, :] = (part[1, top, :] + cr[1, top, :].astype(F32) + r1[top, :].astype(F32)).astype(BF16)
    up3 = ring(4, s2.at[0, top], r2.at[0, top], 1)
    down1.wait_recv()
    s2[1, low, :] = (part[2, low, :] + cr[2, low, :].astype(F32) + r1[low, :].astype(F32)).astype(BF16)
    down3 = ring(5, s2.at[1, low], r2.at[1, low], -1)
    swaps[3].wait_recv()
    part[3] = part[3] + cr[3].astype(F32)
    for copy in (up2, down2, up3, down3):
        copy.wait_recv()
    out_ref[...] = (part[3] + r2[0].astype(F32) + r2[1].astype(F32)).astype(BF16)

    for copy in sent + swaps + [up1, down1, up2, down2, up3, down3]:
        copy.wait_send()


def per_device(outer_gate, inner_gate, values_in, filters, skip_gain, w_out):
    rows, chans = outer_gate.shape
    depth, cols = w_out.shape
    nctx = 16
    hbm = pl.BlockSpec(memory_space=pl.ANY)
    vmem = pl.BlockSpec(memory_space=pltpu.VMEM)
    dma = pltpu.SemaphoreType.DMA
    scratch = [
        pltpu.VMEM((rows, chans), BF16),
        pltpu.VMEM((rows, chans), BF16),
        pltpu.VMEM((rows, chans), BF16),
        pltpu.VMEM((rows, chans), F32),
        pltpu.VMEM((rows, 2 * rows), BF16),
        pltpu.VMEM((2 * rows, 2 * rows), BF16),
        pltpu.VMEM((rows, chans), BF16),
        pltpu.VMEM((chans, rows), BF16),
        pltpu.VMEM((chans, rows), BF16),
        pltpu.VMEM((chans, rows), BF16),
        pltpu.VMEM((chans, rows), BF16),
        pltpu.VMEM((chans, 2 * rows), F32),
        pltpu.VMEM((chans, 2 * rows), F32),
        pltpu.VMEM((chans, 2 * rows), F32),
        pltpu.VMEM((chans, 2 * rows), F32),
        pltpu.VMEM((chans, rows), BF16),
        pltpu.VMEM((chans, rows), BF16),
        pltpu.VMEM((rows, chans), BF16),
        pltpu.VMEM((nctx, depth, cols), BF16),
        pltpu.VMEM((RING, rows, 2 * cols), F32),
        pltpu.VMEM((RING, rows, 2 * cols), BF16),
        pltpu.VMEM((RING, rows, 2 * cols), BF16),
        pltpu.VMEM((rows, 2 * cols), BF16),
        pltpu.VMEM((rows, 2 * cols), BF16),
        pltpu.VMEM((2, rows, 2 * cols), BF16),
        pltpu.VMEM((2, rows, 2 * cols), BF16),
        dma((7,)),
        dma((nctx,)), dma((nctx,)), dma((nctx,)), dma((nctx,)), dma((nctx,)), dma((nctx,)),
        dma((40,)), dma((40,)),
        dma((RING,)), dma((RING,)),
        dma((6,)), dma((6,)),
    ]
    return pl.pallas_call(
        kernel,
        out_shape=jax.ShapeDtypeStruct((rows, chans), BF16),
        in_specs=[hbm, hbm, hbm, hbm, vmem, hbm, hbm, hbm],
        out_specs=vmem,
        scratch_shapes=scratch,
        compiler_params=pltpu.CompilerParams(
            collective_id=0, has_side_effects=True, vmem_limit_bytes=48 * 1024 * 1024
        ),
        name="long_conv_layer",
    )(
        outer_gate, inner_gate, values_in, filters, skip_gain[None, :], w_out,
        jnp.asarray(forward_table(rows)), jnp.asarray(inverse_table(rows)),
    )


def solution(mesh):
    placed = (
        P("ctx", "ch"),
        P("ctx", "ch"),
        P("ctx", "ch"),
        P("ctx", "ch"),
        P("ch"),
        P("ch", "ctx"),
    )
    return jax.shard_map(
        per_device, mesh=mesh, in_specs=placed, out_specs=P("ctx", "ch"), check_vma=False
    )
```

time: 325 us -> 62.7 us (0.19); the launches traced: 320 us -> 62.4 us
  waiting for transfers between devices: 254 us -> 0 us
  Pallas kernels: 0 us -> 54.1 us
  other arithmetic: 22.9 us -> 0 us
  matrix products: 15.8 us -> 0 us
  between operations: 13.2 us -> 0.02 us
  starting transfers between devices: 12.2 us -> 0 us
  local copies, waits for them, and re-layouts: 1.64 us -> 8.22 us
    reduce_scatter x1 -> x0, waiting for transfers between devices: 133 us -> none  [per_device(): lax.psum_scatter(partial_rows.astype(jnp.bfloat16), 'ch', scatter_dimensi...]
    all_gather x3 -> x0, waiting for transfers between devices: 121 us -> none  [the longest x1 46.8 us: per_device(): piece = lax.all_gather(gated[None], 'ctx', axis=0, tiled=True)]
    pallas_call x0 -> x1, Pallas kernels: none -> 54.1 us  [per_device(): pl.pallas_call(kernel, out_shape=jax.ShapeDtypeStruct((rows, chans), BF16...]
    dot_general x5 -> x0, matrix products: 15.8 us -> none  [the longest x1 5.89 us: per_device(): lax.dot_general(inverse, summed, (((0,), (1,)), ((), ())), precision=lax....]
    ppermute x1 -> x0, starting transfers between devices: 12.1 us -> none  [from_behind(): return lax.ppermute(block, axis, route)]
    convert_element_type x4 -> x0, other arithmetic: 11.1 us -> none  [the longest x1 6.63 us: per_device(): lax.all_gather(filters.astype(jnp.bfloat16), 'ctx', axis=0, tiled=True)]
    unnamed x6 -> x17, local copies, waits for them, and re-layouts: 0.02 us -> 8.22 us
    neg x2 -> x0, other arithmetic: 7.06 us -> none  [the longest x1 4.99 us: inverse_table(): return jnp.concatenate([jnp.cos(angles), -jnp.sin(angles)], axis=0) / length]
  transfers between devices with their start and end apart: 5 -> 0, of which waited for: 4 -> 0; matrix products, arithmetic and copies ran while one was open for 11% -> 0% of each run, Pallas kernels for 0% -> 0%
where the time goes in v1:
time: 62.7 us; the launch traced here: 62.4 us
  Pallas kernels  54.1 us (86%)
  local copies, waits for them, and re-layouts  8.22 us (13%)
    pallas_call x1, Pallas kernels, per_device(): pl.pallas_call(kernel, out_shape=jax.ShapeDtypeStruct((rows, chans), BF16...  54.1 us
    unnamed x17, local copies, waits for them, and re-layouts  8.22 us

profile of v1, /device:TPU:1, one launch (start us, length us, event | category | flops | bytes accessed | tf_op | source)
XLA Modules:
  0.0 62.4 jit_solution(15489689135306684864)
XLA Ops:
  0.0 0.0 copy-start
  0.0 1.0 %copy-done = f32[256,512]{1,0:T(8,128)S(1)} copy-done((f32[256,512]{1,0:T(8,128)S(1)}, f32[256,512]{1,0:T(8,128)}, u32[]{:S(2)}) %copy-start) | copy-done | bytes 524312
  1.0 0.0 copy-start.1
  1.0 1.0 %copy-done.1 = bf16[512,512]{1,0:T(8,128)(2,1)S(1)} copy-done((bf16[512,512]{1,0:T(8,128)(2,1)S(1)}, bf16[512,512]{1,0:T(8,128)(2,1)}, u32[]{:S(2)}) %copy-start.1) | copy-done | bytes 524312
  2.1 0.0 copy-start.2
  2.1 0.9 %copy-done.2 = bf16[256,512]{1,0:T(8,128)(2,1)S(1)} copy-done((bf16[256,512]{1,0:T(8,128)(2,1)S(1)}, bf16[256,512]{1,0:T(8,128)(2,1)}, u32[]{:S(2)}) %copy-start.2) | copy-done | bytes 262168
  3.0 0.0 copy-start.3
  3.0 0.9 %copy-done.3 = bf16[256,512]{1,0:T(8,128)(2,1)S(1)} copy-done((bf16[256,512]{1,0:T(8,128)(2,1)S(1)}, bf16[256,512]{1,0:T(8,128)(2,1)}, u32[]{:S(2)}) %copy-start.3) | copy-done | bytes 262168
  4.0 0.0 copy-start.4
  4.0 0.9 %copy-done.4 = bf16[256,512]{1,0:T(8,128)(2,1)S(1)} copy-done((bf16[256,512]{1,0:T(8,128)(2,1)S(1)}, bf16[256,512]{1,0:T(8,128)(2,1)}, u32[]{:S(2)}) %copy-start.4) | copy-done | bytes 262168
  4.9 0.0 copy-start.5
  4.9 0.9 %copy-done.5 = bf16[512,256]{1,0:T(8,128)(2,1)S(1)} copy-done((bf16[512,256]{1,0:T(8,128)(2,1)S(1)}, bf16[512,256]{1,0:T(8,128)(2,1)}, u32[]{:S(2)}) %copy-start.5) | copy-done | bytes 262168
  5.9 0.0 copy-start.6
  5.9 0.9 %copy-done.6 = bf16[256,512]{1,0:T(8,128)(2,1)S(1)} copy-done((bf16[256,512]{1,0:T(8,128)(2,1)S(1)}, bf16[256,512]{1,0:T(8,128)(2,1)}, u32[]{:S(2)}) %copy-start.6) | copy-done | bytes 262168
  6.8 0.0 copy-start.7
  6.8 0.7 %copy-done.7 = f32[512]{0:T(512)S(1)} copy-done((f32[512]{0:T(512)S(1)}, f32[512]{0:T(512)}, u32[]{:S(2)}) %copy-start.7) | copy-done | bytes 2072
  7.5 54.1 %long_conv_layer.1 = bf16[256,512]{1,0:T(8,128)(2,1)S(1)} custom-call(bf16[256,512]{1,0:T(8,128)(2,1)S(1)} %copy-done.2, bf16[256,512]{1,0:T(8,128)(2,1)S(1)} %copy-done.3, bf16[256,512]{1,0:T(8,128)(2,1)S(1)} %copy-done.4, f32[256,512]{1,0:T(8,128)S(1)} %copy-done, f32[1,512]{1,0:T(1,128)S(1)} %bitcast.1, bf16[512,256]{1,0:T(8,128)(2,1)S(1)} %copy-done.5, ...), custom_call_target="tpu_custom_call" | custom-call | tf_op jit(solution)/shard_map/long_conv_layer/pallas_call | solution.py:326
  61.6 0.7 %copy.10 = bf16[256,512]{1,0:T(8,128)(2,1)} copy(bf16[256,512]{1,0:T(8,128)(2,1)S(1)} %long_conv_layer.1) | data formatting | bytes 524288
Async XLA Ops:
  0.0 1.0 %copy-start = (f32[256,512]{1,0:T(8,128)S(1)}, f32[256,512]{1,0:T(8,128)}, u32[]{:S(2)}) copy-start(f32[256,512]{1,0:T(8,128)} %fl_h.1) | copy-start | bytes 1572868
  1.0 1.0 %copy-start.1 = (bf16[512,512]{1,0:T(8,128)(2,1)S(1)}, bf16[512,512]{1,0:T(8,128)(2,1)}, u32[]{:S(2)}) copy-start(bf16[512,512]{1,0:T(8,128)(2,1)} %constant.5.clone.it_h) | copy-start | bytes 1572868
  2.1 0.9 %copy-start.2 = (bf16[256,512]{1,0:T(8,128)(2,1)S(1)}, bf16[256,512]{1,0:T(8,128)(2,1)}, u32[]{:S(2)}) copy-start(bf16[256,512]{1,0:T(8,128)(2,1)} %og_h.1) | copy-start | bytes 786436
  3.0 0.9 %copy-start.3 = (bf16[256,512]{1,0:T(8,128)(2,1)S(1)}, bf16[256,512]{1,0:T(8,128)(2,1)}, u32[]{:S(2)}) copy-start(bf16[256,512]{1,0:T(8,128)(2,1)} %ig_h.1) | copy-start | bytes 786436
  4.0 0.9 %copy-start.4 = (bf16[256,512]{1,0:T(8,128)(2,1)S(1)}, bf16[256,512]{1,0:T(8,128)(2,1)}, u32[]{:S(2)}) copy-start(bf16[256,512]{1,0:T(8,128)(2,1)} %vi_h.1) | copy-start | bytes 786436
  4.9 0.9 %copy-start.5 = (bf16[512,256]{1,0:T(8,128)(2,1)S(1)}, bf16[512,256]{1,0:T(8,128)(2,1)}, u32[]{:S(2)}) copy-start(bf16[512,256]{1,0:T(8,128)(2,1)} %w_h.1) | copy-start | bytes 786436
  5.9 0.9 %copy-start.6 = (bf16[256,512]{1,0:T(8,128)(2,1)S(1)}, bf16[256,512]{1,0:T(8,128)(2,1)}, u32[]{:S(2)}) copy-start(bf16[256,512]{1,0:T(8,128)(2,1)} %constant.4.clone.ft_h) | copy-start | bytes 786436
  6.8 0.7 %copy-start.7 = (f32[512]{0:T(512)S(1)}, f32[512]{0:T(512)}, u32[]{:S(2)}) copy-start(f32[512]{0:T(512)} %param.12) | copy-start | bytes 6148

commit v2 on v1

--- a/solution.py
+++ b/solution.py
@@ -28,8 +28,8 @@
 
 
 def kernel(
-    og_h, ig_h, vi_h, fl_h, sk_ref, w_h, ft_h, it_h, out_ref,
-    og, ig, vi, fl, ft, it, gated, gsend, hsend, gx, hx, gs, hs, ys, ps, csend, cx, mix, wall,
+    og_h, ig_h, vi_h, fl_h, sk_h, w_h, ft_h, it_h, out_ref,
+    og, ig, vi, fl, sk, ft, it, gated, gsend, hsend, gx, hx, gs, hs, ys, ps, csend, cx, mix, wall,
     part, other, cr, s1, r1, s2, r2,
     ld, gsem_s, gsem_r, hsem_s, hsem_r, csem_s, csem_r, wsem_s, wsem_r, osem_s, osem_r, xsem_s, xsem_r,
 ):
@@ -50,7 +50,7 @@
     loads = [
         pltpu.make_async_copy(src, dst, ld.at[n])
         for n, (src, dst) in enumerate(
-            [(ig_h, ig), (vi_h, vi), (fl_h, fl), (w_h, wall.at[me]), (ft_h, ft), (it_h, it), (og_h, og)]
+            [(ig_h, ig), (vi_h, vi), (fl_h, fl), (w_h, wall.at[me]), (ft_h, ft), (it_h, it), (og_h, og), (sk_h, sk)]
         )
     ]
     for copy in loads:
@@ -209,10 +209,11 @@
             w_send(h, 1, ra, "FL")
 
     loads[6].wait()
+    loads[7].wait()
     for d in range(1, nctx):
         exchange_wait(csend, cx, csem_s, csem_r, d)
     conv = jnp.transpose(cx[...].astype(F32))
-    mix[...] = (og[...].astype(F32) * (conv + sk_ref[...] * gated[...].astype(F32))).astype(BF16)
+    mix[...] = (og[...].astype(F32) * (conv + sk[...] * gated[...].astype(F32))).astype(BF16)
 
     for ra in (2,):
         for h in (0, 1):
@@ -295,6 +296,7 @@
         pltpu.VMEM((rows, chans), BF16),
         pltpu.VMEM((rows, chans), BF16),
         pltpu.VMEM((rows, chans), F32),
+        pltpu.VMEM((1, chans), F32),
         pltpu.VMEM((rows, 2 * rows), BF16),
         pltpu.VMEM((2 * rows, 2 * rows), BF16),
         pltpu.VMEM((rows, chans), BF16),
@@ -317,26 +319,27 @@
         pltpu.VMEM((rows, 2 * cols), BF16),
         pltpu.VMEM((2, rows, 2 * cols), BF16),
         pltpu.VMEM((2, rows, 2 * cols), BF16),
-        dma((7,)),
+        dma((8,)),
         dma((nctx,)), dma((nctx,)), dma((nctx,)), dma((nctx,)), dma((nctx,)), dma((nctx,)),
         dma((40,)), dma((40,)),
         dma((RING,)), dma((RING,)),
         dma((6,)), dma((6,)),
     ]
+    operands = (
+        outer_gate, inner_gate, values_in, filters, skip_gain[None, :], w_out,
+        jnp.asarray(forward_table(rows)), jnp.asarray(inverse_table(rows)),
+    )
     return pl.pallas_call(
         kernel,
         out_shape=jax.ShapeDtypeStruct((rows, chans), BF16),
-        in_specs=[hbm, hbm, hbm, hbm, vmem, hbm, hbm, hbm],
+        in_specs=[hbm] * 8,
         out_specs=vmem,
         scratch_shapes=scratch,
         compiler_params=pltpu.CompilerParams(
             collective_id=0, has_side_effects=True, vmem_limit_bytes=48 * 1024 * 1024
         ),
         name="long_conv_layer",
-    )(
-        outer_gate, inner_gate, values_in, filters, skip_gain[None, :], w_out,
-        jnp.asarray(forward_table(rows)), jnp.asarray(inverse_table(rows)),
-    )
+    )(*[pltpu.with_memory_space_constraint(operand, pltpu.HBM) for operand in operands])
 
 
 def solution(mesh):

time: 62.7 us -> 54.8 us (0.87)
  local copies, waits for them, and re-layouts: 8.22 us -> 0.71 us
    unnamed x17 -> x1, local copies, waits for them, and re-layouts: 8.22 us -> 0.71 us
where the time goes in v2:
time: 54.8 us; the launch traced here: 54.7 us
  Pallas kernels  54 us (99%)
  local copies, waits for them, and re-layouts  0.71 us (1%)
    pallas_call x1, Pallas kernels, per_device(): pl.pallas_call(kernel, out_shape=jax.ShapeDtypeStruct((rows, chans), BF16...  54 us

profile of v2, /device:TPU:1, one launch (start us, length us, event | category | flops | bytes accessed | tf_op | source)
XLA Modules:
  0.0 54.7 jit_solution(4246659174143573766)
XLA Ops:
  0.0 54.0 %long_conv_layer.1 = bf16[256,512]{1,0:T(8,128)(2,1)S(1)} custom-call(bf16[256,512]{1,0:T(8,128)(2,1)} %og_h.1, bf16[256,512]{1,0:T(8,128)(2,1)} %ig_h.1, bf16[256,512]{1,0:T(8,128)(2,1)} %vi_h.1, f32[256,512]{1,0:T(8,128)} %fl_h.1, f32[1,512]{1,0:T(1,128)} %bitcast.1, bf16[512,256]{1,0:T(8,128)(2,1)} %w_h.1, bf16[256,512]{1,0:T(8,128)(2,1)} %constant.4.clone.ft_h, ...), custom_call_target="tpu_custom_call" | custom-call | tf_op jit(solution)/shard_map/long_conv_layer/pallas_call | solution.py:332
  54.0 0.7 %copy.10 = bf16[256,512]{1,0:T(8,128)(2,1)} copy(bf16[256,512]{1,0:T(8,128)(2,1)S(1)} %long_conv_layer.1) | data formatting | bytes 524288

commit v3 on v2

--- a/solution.py
+++ b/solution.py
@@ -29,9 +29,9 @@
 
 def kernel(
     og_h, ig_h, vi_h, fl_h, sk_h, w_h, ft_h, it_h, out_ref,
-    og, ig, vi, fl, sk, ft, it, gated, gsend, hsend, gx, hx, gs, hs, ys, ps, csend, cx, mix, wall,
-    part, other, cr, s1, r1, s2, r2,
-    ld, gsem_s, gsem_r, hsem_s, hsem_r, csem_s, csem_r, wsem_s, wsem_r, osem_s, osem_r, xsem_s, xsem_r,
+    og, ig, vi, fl, sk, ft, it, wl, gated, gsend, hsend, gx, hx, gs, hs, ys, ps, csend, cx, mixes, wall,
+    part, other, cr, xs, xr,
+    ld, gsem_s, gsem_r, hsem_s, hsem_r, csem_s, csem_r, wsem_s, wsem_r, psem_s, psem_r, osem_s, osem_r, xsem_s, xsem_r,
 ):
     nctx = 16
     me = lax.axis_index("ctx")
@@ -39,7 +39,10 @@
     y, z = lax.rem(me, RING), me // RING
     x, core = mych // 2, lax.rem(mych, 2)
     sub = gsend.shape[0] // nctx
-    half = w_h.shape[0] // 2
+    depth, cols = w_h.shape[0], w_h.shape[1]
+    side = cols // 2
+    odd = lax.rem(x, 2)
+    partner = x + 1 - 2 * odd
 
     def ctx_of(ry, rz):
         return lax.rem(z + rz + RING, RING) * RING + lax.rem(y + ry + RING, RING)
@@ -50,7 +53,8 @@
     loads = [
         pltpu.make_async_copy(src, dst, ld.at[n])
         for n, (src, dst) in enumerate(
-            [(ig_h, ig), (vi_h, vi), (fl_h, fl), (w_h, wall.at[me]), (ft_h, ft), (it_h, it), (og_h, og), (sk_h, sk)]
+            [(ig_h, ig), (vi_h, vi), (fl_h, fl), (w_h.at[:, pl.ds(pl.multiple_of(odd * side, side), side)], wall.at[me, 0]), (ft_h, ft), (it_h, it), (og_h, og), (sk_h, sk),
+             (w_h.at[:, pl.ds(pl.multiple_of((1 - odd) * side, side), side)], wl)]
         )
     ]
     for copy in loads:
@@ -60,8 +64,8 @@
     for d in range(1, nctx):
         pl.semaphore_signal(barrier, inc=1, device_id={"ctx": lax.rem(me + d, nctx)})
     pl.semaphore_signal(barrier, inc=1, device_id={"ch": ch_of(0, 1 - core)})
-    pl.semaphore_signal(barrier, inc=1, device_id={"ch": ch_of(1, core)})
-    pl.semaphore_signal(barrier, inc=1, device_id={"ch": ch_of(-1, core)})
+    for rx in (1, 2, 3):
+        pl.semaphore_signal(barrier, inc=1, device_id={"ch": ch_of(rx, core)})
 
     sent = []
     kinds = {}
@@ -73,12 +77,12 @@
         n = kinds[key]
         step = 1 if what in ("R", "FR") else -1
         rel = {"R": 0, "L": 0, "FR": -1, "FL": 1}[what]
-        rows = {"R": (0, half), "L": (0, half), "FR": (0, half // 2), "FL": (half // 2, half // 2)}[what]
+        rows = {"R": (0, depth), "L": (0, depth), "FR": (0, depth // 2), "FL": (depth // 2, depth // 2)}[what]
         first, second = (rel, 0) if stage == 0 else (ra, rel)
         chunk = ctx_of(first, second) if h == 0 else ctx_of(second, first)
         along_y = (h == 0) == (stage == 0)
         to = ctx_of(step, 0) if along_y else ctx_of(0, step)
-        ref = wall.at[chunk, pl.ds(h * half + rows[0], rows[1])]
+        ref = wall.at[chunk, h, pl.ds(*rows)]
         return pltpu.make_async_remote_copy(
             src_ref=ref, dst_ref=ref, send_sem=wsem_s.at[n], recv_sem=wsem_r.at[n], device_id={"ctx": to}
         )
@@ -87,12 +91,12 @@
         n = kinds[(h, stage, ra, what)]
         step = 1 if what in ("R", "FR") else -1
         rel = {"R": 0, "L": 0, "FR": -1, "FL": 1}[what] - step
-        rows = {"R": (0, half), "L": (0, half), "FR": (0, half // 2), "FL": (half // 2, half // 2)}[what]
+        rows = {"R": (0, depth), "L": (0, depth), "FR": (0, depth // 2), "FL": (depth // 2, depth // 2)}[what]
         first, second = (rel, 0) if stage == 0 else (ra, rel)
         chunk = ctx_of(first, second) if h == 0 else ctx_of(second, first)
         along_y = (h == 0) == (stage == 0)
         to = ctx_of(step, 0) if along_y else ctx_of(0, step)
-        ref = wall.at[chunk, pl.ds(h * half + rows[0], rows[1])]
+        ref = wall.at[chunk, h, pl.ds(*rows)]
         pltpu.make_async_remote_copy(
             src_ref=ref, dst_ref=ref, send_sem=wsem_s.at[n], recv_sem=wsem_r.at[n], device_id={"ctx": to}
         ).wait_recv()
@@ -136,18 +140,31 @@
     gated[...] = product
     gsend[...] = jnp.transpose(product.astype(F32)).astype(BF16)
     loads[3].wait()
-    pl.semaphore_wait(barrier, nctx + 2)
+    pl.semaphore_wait(barrier, nctx + 3)
+    loads[8].wait()
+
+    def with_partner(n, src, dst):
+        return pltpu.make_async_remote_copy(
+            src_ref=src, dst_ref=dst, send_sem=psem_s.at[n], recv_sem=psem_r.at[n],
+            device_id={"ch": partner * 2 + core},
+        )
+
+    w_pair = with_partner(0, wl, wall.at[me, 1])
+    w_pair.start()
+    sent.append(w_pair)
     exchange_all(gsend, gx, gsem_s, gsem_r)
     loads[2].wait()
     hsend[...] = jnp.transpose(fl[...]).astype(BF16)
     exchange_all(hsend, hx, hsem_s, hsem_r)
-    for h in (0, 1):
-        for what in ("R", "L"):
-            w_send(h, 0, 0, what)
-    for h in (0, 1):
-        for what in ("R", "L"):
-            w_send(h, 1, 0, what)
-
+    for what in ("R", "L"):
+        w_send(0, 0, 0, what)
+    for what in ("R", "L"):
+        w_send(0, 1, 0, what)
+    w_pair.wait_recv()
+    for what in ("R", "L"):
+        w_send(1, 0, 0, what)
+    for what in ("R", "L"):
+        w_send(1, 1, 0, what)
     loads[4].wait()
     for d in range(1, nctx):
         exchange_wait(gsend, gx, gsem_s, gsem_r, d)
@@ -155,16 +172,6 @@
     for d in range(1, nctx):
         exchange_wait(hsend, hx, hsem_s, hsem_r, d)
     hs[...] = jnp.dot(hx[...], ft[...], preferred_element_type=F32)
-
-    for h in (0, 1):
-        w_wait(h, 0, 0, "R")
-        w_send(h, 0, 0, "FR")
-        w_send(h, 1, -1, "R")
-        w_send(h, 1, -1, "L")
-        w_wait(h, 0, 0, "L")
-        w_send(h, 0, 0, "FL")
-        w_send(h, 1, 1, "R")
-        w_send(h, 1, 1, "L")
 
     bins = gs.shape[1] // 2
 
@@ -196,91 +203,140 @@
     ).astype(BF16)
     exchange_all(csend, cx, csem_s, csem_r)
 
-    for h in (0, 1):
-        w_wait(h, 0, 0, "FR")
-        w_wait(h, 0, 0, "FL")
-        w_send(h, 1, 2, "R")
-        w_send(h, 1, 2, "L")
-    for ra in (0, -1, 1):
-        for h in (0, 1):
-            w_wait(h, 1, ra, "R")
-            w_send(h, 1, ra, "FR")
-            w_wait(h, 1, ra, "L")
-            w_send(h, 1, ra, "FL")
+    def relay(h, stage, ra):
+        w_wait(h, stage, ra, "R")
+        w_send(h, stage, ra, "FR")
+        w_wait(h, stage, ra, "L")
+        w_send(h, stage, ra, "FL")
+
+    relay(1, 0, 0)
+    relay(0, 1, 0)
+    relay(0, 0, 0)
+    for ra in (-1, 1):
+        for what in ("R", "L"):
+            for h in (0, 1):
+                w_send(h, 1, ra, what)
 
     loads[6].wait()
     loads[7].wait()
     for d in range(1, nctx):
         exchange_wait(csend, cx, csem_s, csem_r, d)
     conv = jnp.transpose(cx[...].astype(F32))
-    mix[...] = (og[...].astype(F32) * (conv + sk[...] * gated[...].astype(F32))).astype(BF16)
-
-    for ra in (2,):
-        for h in (0, 1):
-            w_wait(h, 1, ra, "R")
-            w_send(h, 1, ra, "FR")
-            w_wait(h, 1, ra, "L")
-            w_send(h, 1, ra, "FL")
-    for ra in (0, -1, 1, 2):
-        for h in (0, 1):
-            w_wait(h, 1, ra, "FR")
-            w_wait(h, 1, ra, "FL")
-
-    cols = w_h.shape[1]
-
-    def columns(rx, c, n):
-        q = lax.rem(x + rx + RING, RING)
-        return jnp.dot(mix[...], wall[q * RING + c * 2 + n], preferred_element_type=F32)
-
+    mixes[0] = (og[...].astype(F32) * (conv + sk[...] * gated[...].astype(F32))).astype(BF16)
+
+    m_pair = with_partner(1, mixes.at[0], mixes.at[1])
+    m_pair.start()
+    sent.append(m_pair)
     turns = (2, 1, -1, 0)
-    swaps = []
-    for k, rx in enumerate(turns):
-        for n in (0, 1):
-            other[k, :, n * cols : (n + 1) * cols] = columns(rx, 1 - core, n).astype(BF16)
-        copy = pltpu.make_async_remote_copy(
-            src_ref=other.at[k], dst_ref=cr.at[k], send_sem=osem_s.at[k], recv_sem=osem_r.at[k],
+
+    def group_of(ry):
+        there = lax.rem(y + ry + RING, RING)
+        return there, there // 2 == core, lax.rem(there, 2)
+
+    def swap(n, k):
+        return pltpu.make_async_remote_copy(
+            src_ref=other.at[n, k], dst_ref=cr.at[n, k],
+            send_sem=osem_s.at[n * RING + k], recv_sem=osem_r.at[n * RING + k],
             device_id={"ch": ch_of(0, 1 - core)},
         )
-        copy.start()
-        swaps.append(copy)
-    for k, rx in enumerate(turns):
-        for n in (0, 1):
-            part[k, :, n * cols : (n + 1) * cols] = columns(rx, core, n)
-
-    rows = mix.shape[0]
-    top, low = pl.ds(0, rows // 2), pl.ds(rows // 2, rows // 2)
-
-    def ring(n, src, dst, step):
-        copy = pltpu.make_async_remote_copy(
-            src_ref=src, dst_ref=dst, send_sem=xsem_s.at[n], recv_sem=xsem_r.at[n],
-            device_id={"ch": ch_of(step, core)},
-        )
-        copy.start()
-        return copy
-
-    swaps[0].wait_recv()
-    s1[...] = (part[0] + cr[0].astype(F32)).astype(BF16)
-    up1 = ring(0, s1.at[top], r1.at[top], 1)
-    down1 = ring(1, s1.at[low], r1.at[low], -1)
-    swaps[1].wait_recv()
-    s2[0, low, :] = (part[1, low, :] + cr[1, low, :].astype(F32)).astype(BF16)
-    up2 = ring(2, s2.at[0, low], r2.at[0, low], 1)
-    swaps[2].wait_recv()
-    s2[1, top, :] = (part[2, top, :] + cr[2, top, :].astype(F32)).astype(BF16)
-    down2 = ring(3, s2.at[1, top], r2.at[1, top], -1)
-    up1.wait_recv()
-    s2[0, top, :] = (part[1, top, :] + cr[1, top, :].astype(F32) + r1[top, :].astype(F32)).astype(BF16)
-    up3 = ring(4, s2.at[0, top], r2.at[0, top], 1)
-    down1.wait_recv()
-    s2[1, low, :] = (part[2, low, :] + cr[2, low, :].astype(F32) + r1[low, :].astype(F32)).astype(BF16)
-    down3 = ring(5, s2.at[1, low], r2.at[1, low], -1)
-    swaps[3].wait_recv()
-    part[3] = part[3] + cr[3].astype(F32)
-    for copy in (up2, down2, up3, down3):
-        copy.wait_recv()
-    out_ref[...] = (part[3] + r2[0].astype(F32) + r2[1].astype(F32)).astype(BF16)
-
-    for copy in sent + swaps + [up1, down1, up2, down2, up3, down3]:
+
+    def share(n, k):
+        return pltpu.make_async_remote_copy(
+            src_ref=xs.at[n, k], dst_ref=xr.at[n, k],
+            send_sem=xsem_s.at[n * RING + k], recv_sem=xsem_r.at[n * RING + k],
+            device_id={"ch": ch_of(turns[k], core)},
+        )
+
+    def multiply(ry):
+        there, mine, n = group_of(ry)
+        for k in (0, 2):
+            value = None
+            for h in (0, 1):
+                two = [wall[lax.rem(x + turns[k + i] + RING, RING) * RING + there, h] for i in (0, 1)]
+                term = jnp.dot(mixes[h], jnp.concatenate(two, axis=1), preferred_element_type=F32)
+                value = term if value is None else value + term
+
+            @pl.when(mine)
+            def _():
+                for i in (0, 1):
+                    part[n, k + i] = value[:, i * side : (i + 1) * side]
+
+            @pl.when(jnp.logical_not(mine))
+            def _():
+                for i in (0, 1):
+                    other[n, k + i] = value[:, i * side : (i + 1) * side].astype(BF16)
+                    swap(n, k + i).start()
+
+    def spread(ry):
+        there, mine, n = group_of(ry)
+
+        @pl.when(mine)
+        def _():
+            for k in range(RING - 1):
+                swap(n, k).wait_recv()
+                xs[n, k] = (part[n, k] + cr[n, k].astype(F32)).astype(BF16)
+                share(n, k).start()
+
+    def finish(ry):
+        there, mine, n = group_of(ry)
+
+        @pl.when(mine)
+        def _():
+            swap(n, RING - 1).wait_recv()
+            total = part[n, RING - 1] + cr[n, RING - 1].astype(F32)
+            for k in range(RING - 1):
+                share(n, k).wait_recv()
+            total += xr[n, 0].astype(F32)
+            beside = xr[n, 1].astype(F32) + xr[n, 2].astype(F32)
+            out_ref[:, pl.ds(pl.multiple_of(n * cols + odd * side, side), side)] = total.astype(BF16)
+            out_ref[:, pl.ds(pl.multiple_of(n * cols + (1 - odd) * side, side), side)] = beside.astype(BF16)
+
+        @pl.when(mine)
+        def _():
+            for k in range(RING - 1):
+                share(n, k).wait_send()
+
+        @pl.when(jnp.logical_not(mine))
+        def _():
+            for k in range(RING):
+                swap(n, k).wait_send()
+
+    for what in ("FR", "FL"):
+        w_wait(1, 0, 0, what)
+        w_wait(0, 1, 0, what)
+    m_pair.wait_recv()
+    multiply(0)
+    for what in ("R", "L"):
+        w_send(1, 1, 2, what)
+    for ra in (-1, 1):
+        relay(0, 1, ra)
+    for what in ("FR", "FL"):
+        w_wait(0, 0, 0, what)
+    for what in ("R", "L"):
+        w_send(0, 1, 2, what)
+    spread(0)
+    for ra in (0, -1, 1):
+        relay(1, 1, ra)
+    finish(0)
+    for ra in (-1, 1):
+        for what in ("FR", "FL"):
+            w_wait(0, 1, ra, what)
+    relay(1, 1, 2)
+    multiply(-1)
+    multiply(1)
+    relay(0, 1, 2)
+    spread(-1)
+    spread(1)
+    for what in ("FR", "FL"):
+        w_wait(0, 1, 2, what)
+        for ra in (0, -1, 1, 2):
+            w_wait(1, 1, ra, what)
+    multiply(2)
+    spread(2)
+    finish(-1)
+    finish(1)
+    finish(2)
+    for copy in sent:
         copy.wait_send()
 
 
@@ -299,6 +355,7 @@
         pltpu.VMEM((1, chans), F32),
         pltpu.VMEM((rows, 2 * rows), BF16),
         pltpu.VMEM((2 * rows, 2 * rows), BF16),
+        pltpu.VMEM((depth, cols // 2), BF16),
         pltpu.VMEM((rows, chans), BF16),
         pltpu.VMEM((chans, rows), BF16),
         pltpu.VMEM((chans, rows), BF16),
@@ -310,20 +367,19 @@
         pltpu.VMEM((chans, 2 * rows), F32),
         pltpu.VMEM((chans, rows), BF16),
         pltpu.VMEM((chans, rows), BF16),
-        pltpu.VMEM((rows, chans), BF16),
-        pltpu.VMEM((nctx, depth, cols), BF16),
-        pltpu.VMEM((RING, rows, 2 * cols), F32),
-        pltpu.VMEM((RING, rows, 2 * cols), BF16),
-        pltpu.VMEM((RING, rows, 2 * cols), BF16),
-        pltpu.VMEM((rows, 2 * cols), BF16),
-        pltpu.VMEM((rows, 2 * cols), BF16),
-        pltpu.VMEM((2, rows, 2 * cols), BF16),
-        pltpu.VMEM((2, rows, 2 * cols), BF16),
-        dma((8,)),
+        pltpu.VMEM((2, rows, chans), BF16),
+        pltpu.VMEM((nctx, 2, depth, cols // 2), BF16),
+        pltpu.VMEM((2, RING, rows, cols // 2), F32),
+        pltpu.VMEM((2, RING, rows, cols // 2), BF16),
+        pltpu.VMEM((2, RING, rows, cols // 2), BF16),
+        pltpu.VMEM((2, RING, rows, cols // 2), BF16),
+        pltpu.VMEM((2, RING, rows, cols // 2), BF16),
+        dma((9,)),
         dma((nctx,)), dma((nctx,)), dma((nctx,)), dma((nctx,)), dma((nctx,)), dma((nctx,)),
         dma((40,)), dma((40,)),
-        dma((RING,)), dma((RING,)),
-        dma((6,)), dma((6,)),
+        dma((2,)), dma((2,)),
+        dma((2 * RING,)), dma((2 * RING,)),
+        dma((2 * RING,)), dma((2 * RING,)),
     ]
     operands = (
         outer_gate, inner_gate, values_in, filters, skip_gain[None, :], w_out,

time: 54.8 us -> 52.6 us (0.960)
  Pallas kernels: 54 us -> 51.7 us
    pallas_call x1, Pallas kernels: 54 us -> 51.7 us  [per_device(): pl.pallas_call(kernel, out_shape=jax.ShapeDtypeStruct((rows, chans), BF16...]
where the time goes in v3:
time: 52.6 us; the launch traced here: 52.4 us
  Pallas kernels  51.7 us (98%)
  local copies, waits for them, and re-layouts  0.71 us (1%)
    pallas_call x1, Pallas kernels, per_device(): pl.pallas_call(kernel, out_shape=jax.ShapeDtypeStruct((rows, chans), BF16...  51.7 us

profile of v3, /device:TPU:1, one launch (start us, length us, event | category | flops | bytes accessed | tf_op | source)
XLA Modules:
  0.0 52.4 jit_solution(2238529108712634955)
XLA Ops:
  0.0 51.7 %long_conv_layer.1 = bf16[256,512]{1,0:T(8,128)(2,1)S(1)} custom-call(bf16[256,512]{1,0:T(8,128)(2,1)} %og_h.1, bf16[256,512]{1,0:T(8,128)(2,1)} %ig_h.1, bf16[256,512]{1,0:T(8,128)(2,1)} %vi_h.1, f32[256,512]{1,0:T(8,128)} %fl_h.1, f32[1,512]{1,0:T(1,128)} %bitcast.1, bf16[512,256]{1,0:T(8,128)(2,1)} %w_h.1, bf16[256,512]{1,0:T(8,128)(2,1)} %constant.4.clone.ft_h, ...), custom_call_target="tpu_custom_call" | custom-call | tf_op jit(solution)/shard_map/long_conv_layer/pallas_call | solution.py:388
  51.7 0.7 %copy.10 = bf16[256,512]{1,0:T(8,128)(2,1)} copy(bf16[256,512]{1,0:T(8,128)(2,1)S(1)} %long_conv_layer.1) | data formatting | bytes 524288

commit v4 on v3

--- a/solution.py
+++ b/solution.py
@@ -303,28 +303,28 @@
 
     for what in ("FR", "FL"):
         w_wait(1, 0, 0, what)
+    for what in ("R", "L"):
+        w_send(1, 1, 2, what)
+    for what in ("FR", "FL"):
         w_wait(0, 1, 0, what)
     m_pair.wait_recv()
     multiply(0)
-    for what in ("R", "L"):
-        w_send(1, 1, 2, what)
     for ra in (-1, 1):
         relay(0, 1, ra)
     for what in ("FR", "FL"):
         w_wait(0, 0, 0, what)
     for what in ("R", "L"):
         w_send(0, 1, 2, what)
-    spread(0)
     for ra in (0, -1, 1):
         relay(1, 1, ra)
-    finish(0)
+    spread(0)
+    relay(1, 1, 2)
+    relay(0, 1, 2)
     for ra in (-1, 1):
         for what in ("FR", "FL"):
             w_wait(0, 1, ra, what)
-    relay(1, 1, 2)
     multiply(-1)
     multiply(1)
-    relay(0, 1, 2)
     spread(-1)
     spread(1)
     for what in ("FR", "FL"):
@@ -333,6 +333,7 @@
             w_wait(1, 1, ra, what)
     multiply(2)
     spread(2)
+    finish(0)
     finish(-1)
     finish(1)
     finish(2)

time: 52.6 us -> 51.3 us (0.975)
  Pallas kernels: 51.7 us -> 50.4 us
    pallas_call x1, Pallas kernels: 51.7 us -> 50.4 us  [per_device(): pl.pallas_call(kernel, out_shape=jax.ShapeDtypeStruct((rows, chans), BF16...]
where the time goes in v4:
time: 51.3 us; the launch traced here: 51.1 us
  Pallas kernels  50.4 us (98%)
  local copies, waits for them, and re-layouts  0.71 us (1%)
    pallas_call x1, Pallas kernels, per_device(): pl.pallas_call(kernel, out_shape=jax.ShapeDtypeStruct((rows, chans), BF16...  50.4 us

profile of v4, /device:TPU:1, one launch (start us, length us, event | category | flops | bytes accessed | tf_op | source)
XLA Modules:
  0.0 51.1 jit_solution(17246460640902519558)
XLA Ops:
  0.0 50.4 %long_conv_layer.1 = bf16[256,512]{1,0:T(8,128)(2,1)S(1)} custom-call(bf16[256,512]{1,0:T(8,128)(2,1)} %og_h.1, bf16[256,512]{1,0:T(8,128)(2,1)} %ig_h.1, bf16[256,512]{1,0:T(8,128)(2,1)} %vi_h.1, f32[256,512]{1,0:T(8,128)} %fl_h.1, f32[1,512]{1,0:T(1,128)} %bitcast.1, bf16[512,256]{1,0:T(8,128)(2,1)} %w_h.1, bf16[256,512]{1,0:T(8,128)(2,1)} %constant.4.clone.ft_h, ...), custom_call_target="tpu_custom_call" | custom-call | tf_op jit(solution)/shard_map/long_conv_layer/pallas_call | solution.py:389
  50.4 0.7 %copy.10 = bf16[256,512]{1,0:T(8,128)(2,1)} copy(bf16[256,512]{1,0:T(8,128)(2,1)S(1)} %long_conv_layer.1) | data formatting | bytes 524288

commit v5 on v4

--- a/solution.py
+++ b/solution.py
@@ -31,7 +31,7 @@
     og_h, ig_h, vi_h, fl_h, sk_h, w_h, ft_h, it_h, out_ref,
     og, ig, vi, fl, sk, ft, it, wl, gated, gsend, hsend, gx, hx, gs, hs, ys, ps, csend, cx, mixes, wall,
     part, other, cr, xs, xr,
-    ld, gsem_s, gsem_r, hsem_s, hsem_r, csem_s, csem_r, wsem_s, wsem_r, psem_s, psem_r, osem_s, osem_r, xsem_s, xsem_r,
+    ld, esem_s, esem_r, wsem_s, wsem_r, psem_s, psem_r, osem_s, osem_r, xsem_s, xsem_r,
 ):
     nctx = 16
     me = lax.axis_index("ctx")
@@ -44,8 +44,11 @@
     odd = lax.rem(x, 2)
     partner = x + 1 - 2 * odd
 
+    along_y = [lax.rem(y + r, RING) for r in range(RING)]
+    along_z = [lax.rem(z + r, RING) * RING for r in range(RING)]
+
     def ctx_of(ry, rz):
-        return lax.rem(z + rz + RING, RING) * RING + lax.rem(y + ry + RING, RING)
+        return along_z[rz % RING] + along_y[ry % RING]
 
     def ch_of(rx, c):
         return lax.rem(x + rx + RING, RING) * 2 + c
@@ -61,8 +64,9 @@
         copy.start()
 
     barrier = pltpu.get_barrier_semaphore()
-    for d in range(1, nctx):
-        pl.semaphore_signal(barrier, inc=1, device_id={"ctx": lax.rem(me + d, nctx)})
+    others = [(ry, rz) for ry in (2, 1, 3, 0) for rz in (2, 1, 3, 0) if (ry, rz) != (0, 0)]
+    for ry, rz in others:
+        pl.semaphore_signal(barrier, inc=1, device_id={"ctx": ctx_of(ry, rz)})
     pl.semaphore_signal(barrier, inc=1, device_id={"ch": ch_of(0, 1 - core)})
     for rx in (1, 2, 3):
         pl.semaphore_signal(barrier, inc=1, device_id={"ch": ch_of(rx, core)})
@@ -80,11 +84,10 @@
         rows = {"R": (0, depth), "L": (0, depth), "FR": (0, depth // 2), "FL": (depth // 2, depth // 2)}[what]
         first, second = (rel, 0) if stage == 0 else (ra, rel)
         chunk = ctx_of(first, second) if h == 0 else ctx_of(second, first)
-        along_y = (h == 0) == (stage == 0)
-        to = ctx_of(step, 0) if along_y else ctx_of(0, step)
+        to = ctx_of(step, 0) if (h == 0) == (stage == 0) else ctx_of(0, step)
         ref = wall.at[chunk, h, pl.ds(*rows)]
         return pltpu.make_async_remote_copy(
-            src_ref=ref, dst_ref=ref, send_sem=wsem_s.at[n], recv_sem=wsem_r.at[n], device_id={"ctx": to}
+            src_ref=ref, dst_ref=ref, send_sem=wsem_s.at[0], recv_sem=wsem_r.at[n], device_id={"ctx": to}
         )
 
     def w_wait(h, stage, ra, what):
@@ -94,45 +97,31 @@
         rows = {"R": (0, depth), "L": (0, depth), "FR": (0, depth // 2), "FL": (depth // 2, depth // 2)}[what]
         first, second = (rel, 0) if stage == 0 else (ra, rel)
         chunk = ctx_of(first, second) if h == 0 else ctx_of(second, first)
-        along_y = (h == 0) == (stage == 0)
-        to = ctx_of(step, 0) if along_y else ctx_of(0, step)
+        to = ctx_of(step, 0) if (h == 0) == (stage == 0) else ctx_of(0, step)
         ref = wall.at[chunk, h, pl.ds(*rows)]
         pltpu.make_async_remote_copy(
-            src_ref=ref, dst_ref=ref, send_sem=wsem_s.at[n], recv_sem=wsem_r.at[n], device_id={"ctx": to}
+            src_ref=ref, dst_ref=ref, send_sem=wsem_s.at[0], recv_sem=wsem_r.at[n], device_id={"ctx": to}
         ).wait_recv()
 
     def w_send(h, stage, ra, what):
-        copy = w_copy(h, stage, ra, what)
-        copy.start()
-        sent.append(copy)
-
-    def exchange(src, dst, ssem, rsem, d):
-        to = lax.rem(me + d, nctx)
+        w_copy(h, stage, ra, what).start()
+
+    def exchange(src, dst, n):
+        mine = pl.ds(pl.multiple_of(me * sub, sub), sub)
+        for ry, rz in others:
+            to = ctx_of(ry, rz)
+            pltpu.make_async_remote_copy(
+                src_ref=src.at[pl.ds(pl.multiple_of(to * sub, sub), sub)], dst_ref=dst.at[mine],
+                send_sem=esem_s.at[n], recv_sem=esem_r.at[n], device_id={"ctx": to},
+            ).start()
+        dst[mine, :] = src[mine, :]
+
+    def exchanged(src, dst, n):
+        rest = pl.ds(0, (nctx - 1) * sub)
         return pltpu.make_async_remote_copy(
-            src_ref=src.at[pl.ds(pl.multiple_of(to * sub, sub), sub)],
-            dst_ref=dst.at[pl.ds(pl.multiple_of(me * sub, sub), sub)],
-            send_sem=ssem.at[d],
-            recv_sem=rsem.at[d],
-            device_id={"ctx": to},
-        )
-
-    def exchange_wait(src, dst, ssem, rsem, d):
-        frm = lax.rem(me - d + nctx, nctx)
-        pltpu.make_async_remote_copy(
-            src_ref=src.at[pl.ds(pl.multiple_of(frm * sub, sub), sub)],
-            dst_ref=dst.at[pl.ds(pl.multiple_of(frm * sub, sub), sub)],
-            send_sem=ssem.at[d],
-            recv_sem=rsem.at[d],
-            device_id={"ctx": frm},
-        ).wait_recv()
-
-    def exchange_all(src, dst, ssem, rsem):
-        for d in range(1, nctx):
-            copy = exchange(src, dst, ssem, rsem, d)
-            copy.start()
-            sent.append(copy)
-        mine = pl.ds(pl.multiple_of(me * sub, sub), sub)
-        dst[mine, :] = src[mine, :]
+            src_ref=src.at[rest], dst_ref=dst.at[rest], send_sem=esem_s.at[n], recv_sem=esem_r.at[n],
+            device_id={"ctx": lax.rem(me + 1, nctx)},
+        )
 
     loads[0].wait()
     loads[1].wait()
@@ -152,10 +141,10 @@
     w_pair = with_partner(0, wl, wall.at[me, 1])
     w_pair.start()
     sent.append(w_pair)
-    exchange_all(gsend, gx, gsem_s, gsem_r)
+    exchange(gsend, gx, 0)
     loads[2].wait()
     hsend[...] = jnp.transpose(fl[...]).astype(BF16)
-    exchange_all(hsend, hx, hsem_s, hsem_r)
+    exchange(hsend, hx, 1)
     for what in ("R", "L"):
         w_send(0, 0, 0, what)
     for what in ("R", "L"):
@@ -166,11 +155,9 @@
     for what in ("R", "L"):
         w_send(1, 1, 0, what)
     loads[4].wait()
-    for d in range(1, nctx):
-        exchange_wait(gsend, gx, gsem_s, gsem_r, d)
+    exchanged(gsend, gx, 0).wait_recv()
     gs[...] = jnp.dot(gx[...], ft[...], preferred_element_type=F32)
-    for d in range(1, nctx):
-        exchange_wait(hsend, hx, hsem_s, hsem_r, d)
+    exchanged(hsend, hx, 1).wait_recv()
     hs[...] = jnp.dot(hx[...], ft[...], preferred_element_type=F32)
 
     bins = gs.shape[1] // 2
@@ -201,7 +188,7 @@
     csend[pl.ds(sub, rest), :] = (
         ps[pl.ds(sub, rest), pl.ds(0, bins)] + ps[pl.ds(0, rest), pl.ds(bins, bins)]
     ).astype(BF16)
-    exchange_all(csend, cx, csem_s, csem_r)
+    exchange(csend, cx, 2)
 
     def relay(h, stage, ra):
         w_wait(h, stage, ra, "R")
@@ -219,8 +206,7 @@
 
     loads[6].wait()
     loads[7].wait()
-    for d in range(1, nctx):
-        exchange_wait(csend, cx, csem_s, csem_r, d)
+    exchanged(csend, cx, 2).wait_recv()
     conv = jnp.transpose(cx[...].astype(F32))
     mixes[0] = (og[...].astype(F32) * (conv + sk[...] * gated[...].astype(F32))).astype(BF16)
 
@@ -230,7 +216,7 @@
     turns = (2, 1, -1, 0)
 
     def group_of(ry):
-        there = lax.rem(y + ry + RING, RING)
+        there = along_y[ry % RING]
         return there, there // 2 == core, lax.rem(there, 2)
 
     def swap(n, k):
@@ -306,17 +292,17 @@
     for what in ("R", "L"):
         w_send(1, 1, 2, what)
     for what in ("FR", "FL"):
+        w_wait(0, 0, 0, what)
+    for what in ("R", "L"):
+        w_send(0, 1, 2, what)
+    for ra in (-1, 1):
+        relay(0, 1, ra)
+    for ra in (0, -1, 1):
+        relay(1, 1, ra)
+    for what in ("FR", "FL"):
         w_wait(0, 1, 0, what)
     m_pair.wait_recv()
     multiply(0)
-    for ra in (-1, 1):
-        relay(0, 1, ra)
-    for what in ("FR", "FL"):
-        w_wait(0, 0, 0, what)
-    for what in ("R", "L"):
-        w_send(0, 1, 2, what)
-    for ra in (0, -1, 1):
-        relay(1, 1, ra)
     spread(0)
     relay(1, 1, 2)
     relay(0, 1, 2)
@@ -327,6 +313,11 @@
     multiply(1)
     spread(-1)
     spread(1)
+    exchanged(gsend, gx, 0).wait_send()
+    exchanged(hsend, hx, 1).wait_send()
+    exchanged(csend, cx, 2).wait_send()
+    for copy in sent:
+        copy.wait_send()
     for what in ("FR", "FL"):
         w_wait(0, 1, 2, what)
         for ra in (0, -1, 1, 2):
@@ -337,8 +328,10 @@
     finish(-1)
     finish(1)
     finish(2)
-    for copy in sent:
-        copy.wait_send()
+    pltpu.make_async_remote_copy(
+        src_ref=wall.at[pl.ds(0, nctx - 1)], dst_ref=wall.at[pl.ds(0, nctx - 1)], send_sem=wsem_s.at[0],
+        recv_sem=wsem_r.at[0], device_id={"ctx": ctx_of(1, 0)},
+    ).wait_send()
 
 
 def per_device(outer_gate, inner_gate, values_in, filters, skip_gain, w_out):
@@ -376,8 +369,8 @@
         pltpu.VMEM((2, RING, rows, cols // 2), BF16),
         pltpu.VMEM((2, RING, rows, cols // 2), BF16),
         dma((9,)),
-        dma((nctx,)), dma((nctx,)), dma((nctx,)), dma((nctx,)), dma((nctx,)), dma((nctx,)),
-        dma((40,)), dma((40,)),
+        dma((3,)), dma((3,)),
+        dma((1,)), dma((40,)),
         dma((2,)), dma((2,)),
         dma((2 * RING,)), dma((2 * RING,)),
         dma((2 * RING,)), dma((2 * RING,)),

time: 51.3 us -> 49.2 us (0.959)
  Pallas kernels: 50.4 us -> 48.3 us
    pallas_call x1, Pallas kernels: 50.4 us -> 48.3 us  [per_device(): pl.pallas_call(kernel, out_shape=jax.ShapeDtypeStruct((rows, chans), BF16...]
where the time goes in v5:
time: 49.2 us; the launch traced here: 49.1 us
  Pallas kernels  48.3 us (98%)
  local copies, waits for them, and re-layouts  0.71 us (1%)
    pallas_call x1, Pallas kernels, per_device(): pl.pallas_call(kernel, out_shape=jax.ShapeDtypeStruct((rows, chans), BF16...  48.3 us

profile of v5, /device:TPU:1, one launch (start us, length us, event | category | flops | bytes accessed | tf_op | source)
XLA Modules:
  0.0 49.1 jit_solution(17423209636094384429)
XLA Ops:
  0.0 48.3 %long_conv_layer.1 = bf16[256,512]{1,0:T(8,128)(2,1)S(1)} custom-call(bf16[256,512]{1,0:T(8,128)(2,1)} %og_h.1, bf16[256,512]{1,0:T(8,128)(2,1)} %ig_h.1, bf16[256,512]{1,0:T(8,128)(2,1)} %vi_h.1, f32[256,512]{1,0:T(8,128)} %fl_h.1, f32[1,512]{1,0:T(1,128)} %bitcast.1, bf16[512,256]{1,0:T(8,128)(2,1)} %w_h.1, bf16[256,512]{1,0:T(8,128)(2,1)} %constant.4.clone.ft_h, ...), custom_call_target="tpu_custom_call" | custom-call | tf_op jit(solution)/shard_map/long_conv_layer/pallas_call | solution.py:382
  48.3 0.7 %copy.10 = bf16[256,512]{1,0:T(8,128)(2,1)} copy(bf16[256,512]{1,0:T(8,128)(2,1)S(1)} %long_conv_layer.1) | data formatting | bytes 524288

commit v6 on v5

--- a/solution.py
+++ b/solution.py
@@ -30,7 +30,7 @@
 def kernel(
     og_h, ig_h, vi_h, fl_h, sk_h, w_h, ft_h, it_h, out_ref,
     og, ig, vi, fl, sk, ft, it, wl, gated, gsend, hsend, gx, hx, gs, hs, ys, ps, csend, cx, mixes, wall,
-    part, other, cr, xs, xr,
+    part, other, cr, xs, xr, early,
     ld, esem_s, esem_r, wsem_s, wsem_r, psem_s, psem_r, osem_s, osem_r, xsem_s, xsem_r,
 ):
     nctx = 16
@@ -64,7 +64,7 @@
         copy.start()
 
     barrier = pltpu.get_barrier_semaphore()
-    others = [(ry, rz) for ry in (2, 1, 3, 0) for rz in (2, 1, 3, 0) if (ry, rz) != (0, 0)]
+    others = [(2, 2), (1, 2), (2, 1), (2, 3), (3, 2), (0, 2), (1, 1), (1, 3), (2, 0), (3, 1), (3, 3), (0, 1), (0, 3), (1, 0), (3, 0)]
     for ry, rz in others:
         pl.semaphore_signal(barrier, inc=1, device_id={"ctx": ctx_of(ry, rz)})
     pl.semaphore_signal(barrier, inc=1, device_id={"ch": ch_of(0, 1 - core)})
@@ -220,8 +220,9 @@
         return there, there // 2 == core, lax.rem(there, 2)
 
     def swap(n, k):
+        two = pl.ds(k, 2)
         return pltpu.make_async_remote_copy(
-            src_ref=other.at[n, k], dst_ref=cr.at[n, k],
+            src_ref=other.at[n, two], dst_ref=cr.at[n, two],
             send_sem=osem_s.at[n * RING + k], recv_sem=osem_r.at[n * RING + k],
             device_id={"ch": ch_of(0, 1 - core)},
         )
@@ -232,6 +233,31 @@
             send_sem=xsem_s.at[n * RING + k], recv_sem=xsem_r.at[n * RING + k],
             device_id={"ch": ch_of(turns[k], core)},
         )
+
+    near_n = 1 - lax.rem(y, 2)
+
+    def multiply_near(mine):
+        there = (core if mine else 1 - core) * 2 + near_n
+        for k in (0, 2):
+            value = None
+            for h in (0, 1):
+                two = [wall[lax.rem(x + turns[k + i] + RING, RING) * RING + there, h] for i in (0, 1)]
+                term = jnp.dot(mixes[h], jnp.concatenate(two, axis=1), preferred_element_type=F32)
+                value = term if value is None else value + term
+            for i in (0, 1):
+                if mine:
+                    part[near_n, k + i] = value[:, i * side : (i + 1) * side]
+                else:
+                    other[near_n, k + i] = value[:, i * side : (i + 1) * side].astype(BF16)
+            if not mine:
+                swap(near_n, k).start()
+
+    def pass_on(n):
+        for k in range(RING - 1):
+            if k % 2 == 0:
+                swap(n, k).wait_recv()
+            xs[n, k] = (part[n, k] + cr[n, k].astype(F32)).astype(BF16)
+            share(n, k).start()
 
     def multiply(ry):
         there, mine, n = group_of(ry)
@@ -251,31 +277,30 @@
             def _():
                 for i in (0, 1):
                     other[n, k + i] = value[:, i * side : (i + 1) * side].astype(BF16)
-                    swap(n, k + i).start()
+                swap(n, k).start()
 
     def spread(ry):
         there, mine, n = group_of(ry)
 
         @pl.when(mine)
         def _():
-            for k in range(RING - 1):
-                swap(n, k).wait_recv()
-                xs[n, k] = (part[n, k] + cr[n, k].astype(F32)).astype(BF16)
-                share(n, k).start()
+            pass_on(n)
+
+    def collect(n):
+        total = part[n, RING - 1] + cr[n, RING - 1].astype(F32)
+        for k in range(RING - 1):
+            share(n, k).wait_recv()
+        total += xr[n, 0].astype(F32)
+        beside = xr[n, 1].astype(F32) + xr[n, 2].astype(F32)
+        out_ref[:, pl.ds(pl.multiple_of(n * cols + odd * side, side), side)] = total.astype(BF16)
+        out_ref[:, pl.ds(pl.multiple_of(n * cols + (1 - odd) * side, side), side)] = beside.astype(BF16)
 
     def finish(ry):
         there, mine, n = group_of(ry)
 
         @pl.when(mine)
         def _():
-            swap(n, RING - 1).wait_recv()
-            total = part[n, RING - 1] + cr[n, RING - 1].astype(F32)
-            for k in range(RING - 1):
-                share(n, k).wait_recv()
-            total += xr[n, 0].astype(F32)
-            beside = xr[n, 1].astype(F32) + xr[n, 2].astype(F32)
-            out_ref[:, pl.ds(pl.multiple_of(n * cols + odd * side, side), side)] = total.astype(BF16)
-            out_ref[:, pl.ds(pl.multiple_of(n * cols + (1 - odd) * side, side), side)] = beside.astype(BF16)
+            collect(n)
 
         @pl.when(mine)
         def _():
@@ -284,7 +309,7 @@
 
         @pl.when(jnp.logical_not(mine))
         def _():
-            for k in range(RING):
+            for k in (0, 2):
                 swap(n, k).wait_send()
 
     for what in ("FR", "FL"):
@@ -309,24 +334,48 @@
     for ra in (-1, 1):
         for what in ("FR", "FL"):
             w_wait(0, 1, ra, what)
-    multiply(-1)
-    multiply(1)
-    spread(-1)
-    spread(1)
+    multiply_near(False)
+    multiply_near(True)
+    pass_on(near_n)
     exchanged(gsend, gx, 0).wait_send()
     exchanged(hsend, hx, 1).wait_send()
     exchanged(csend, cx, 2).wait_send()
     for copy in sent:
         copy.wait_send()
+    there, mine, n = group_of(2)
+
+    def last_term(h, k):
+        two = [wall[lax.rem(x + turns[k + i] + RING, RING) * RING + there, h] for i in (0, 1)]
+        return jnp.dot(mixes[h], jnp.concatenate(two, axis=1), preferred_element_type=F32)
+
     for what in ("FR", "FL"):
         w_wait(0, 1, 2, what)
+    early[0] = last_term(0, 0)
+    early[1] = last_term(0, 2)
+    for what in ("FR", "FL"):
         for ra in (0, -1, 1, 2):
             w_wait(1, 1, ra, what)
-    multiply(2)
+    for k in (0, 2):
+        value = early[k // 2] + last_term(1, k)
+
+        @pl.when(mine)
+        def _():
+            for i in (0, 1):
+                part[n, k + i] = value[:, i * side : (i + 1) * side]
+
+        @pl.when(jnp.logical_not(mine))
+        def _():
+            for i in (0, 1):
+                other[n, k + i] = value[:, i * side : (i + 1) * side].astype(BF16)
+            swap(n, k).start()
+
     spread(2)
     finish(0)
-    finish(-1)
-    finish(1)
+    collect(near_n)
+    for k in (0, 2):
+        swap(near_n, k).wait_send()
+    for k in range(RING - 1):
+        share(near_n, k).wait_send()
     finish(2)
     pltpu.make_async_remote_copy(
         src_ref=wall.at[pl.ds(0, nctx - 1)], dst_ref=wall.at[pl.ds(0, nctx - 1)], send_sem=wsem_s.at[0],
@@ -368,6 +417,7 @@
         pltpu.VMEM((2, RING, rows, cols // 2), BF16),
         pltpu.VMEM((2, RING, rows, cols // 2), BF16),
         pltpu.VMEM((2, RING, rows, cols // 2), BF16),
+        pltpu.VMEM((2, rows, cols), F32),
         dma((9,)),
         dma((3,)), dma((3,)),
         dma((1,)), dma((40,)),

time: 49.2 us -> 49.1 us (level)
  no operation moved by 1% of the time
where the time goes in v6:
time: 49.1 us; the launch traced here: 48.9 us
  Pallas kernels  48.2 us (98%)
  local copies, waits for them, and re-layouts  0.71 us (1%)
    pallas_call x1, Pallas kernels, per_device(): pl.pallas_call(kernel, out_shape=jax.ShapeDtypeStruct((rows, chans), BF16...  48.2 us

profile of v6, /device:TPU:1, one launch (start us, length us, event | category | flops | bytes accessed | tf_op | source)
XLA Modules:
  0.0 48.9 jit_solution(4675061433894113363)
XLA Ops:
  0.0 48.2 %long_conv_layer.1 = bf16[256,512]{1,0:T(8,128)(2,1)S(1)} custom-call(bf16[256,512]{1,0:T(8,128)(2,1)} %og_h.1, bf16[256,512]{1,0:T(8,128)(2,1)} %ig_h.1, bf16[256,512]{1,0:T(8,128)(2,1)} %vi_h.1, f32[256,512]{1,0:T(8,128)} %fl_h.1, f32[1,512]{1,0:T(1,128)} %bitcast.1, bf16[512,256]{1,0:T(8,128)(2,1)} %w_h.1, bf16[256,512]{1,0:T(8,128)(2,1)} %constant.4.clone.ft_h, ...), custom_call_target="tpu_custom_call" | custom-call | tf_op jit(solution)/shard_map/long_conv_layer/pallas_call | solution.py:432
  48.2 0.7 %copy.10 = bf16[256,512]{1,0:T(8,128)(2,1)} copy(bf16[256,512]{1,0:T(8,128)(2,1)S(1)} %long_conv_layer.1) | data formatting | bytes 524288

commit v7 on v6

--- a/solution.py
+++ b/solution.py
@@ -30,7 +30,7 @@
 def kernel(
     og_h, ig_h, vi_h, fl_h, sk_h, w_h, ft_h, it_h, out_ref,
     og, ig, vi, fl, sk, ft, it, wl, gated, gsend, hsend, gx, hx, gs, hs, ys, ps, csend, cx, mixes, wall,
-    part, other, cr, xs, xr, early,
+    part, other, cr, xs, xr,
     ld, esem_s, esem_r, wsem_s, wsem_r, psem_s, psem_r, osem_s, osem_r, xsem_s, xsem_r,
 ):
     nctx = 16
@@ -53,16 +53,6 @@
     def ch_of(rx, c):
         return lax.rem(x + rx + RING, RING) * 2 + c
 
-    loads = [
-        pltpu.make_async_copy(src, dst, ld.at[n])
-        for n, (src, dst) in enumerate(
-            [(ig_h, ig), (vi_h, vi), (fl_h, fl), (w_h.at[:, pl.ds(pl.multiple_of(odd * side, side), side)], wall.at[me, 0]), (ft_h, ft), (it_h, it), (og_h, og), (sk_h, sk),
-             (w_h.at[:, pl.ds(pl.multiple_of((1 - odd) * side, side), side)], wl)]
-        )
-    ]
-    for copy in loads:
-        copy.start()
-
     barrier = pltpu.get_barrier_semaphore()
     others = [(2, 2), (1, 2), (2, 1), (2, 3), (3, 2), (0, 2), (1, 1), (1, 3), (2, 0), (3, 1), (3, 3), (0, 1), (0, 3), (1, 0), (3, 0)]
     for ry, rz in others:
@@ -70,6 +60,16 @@
     pl.semaphore_signal(barrier, inc=1, device_id={"ch": ch_of(0, 1 - core)})
     for rx in (1, 2, 3):
         pl.semaphore_signal(barrier, inc=1, device_id={"ch": ch_of(rx, core)})
+
+    loads = [
+        pltpu.make_async_copy(src, dst, ld.at[n])
+        for n, (src, dst) in enumerate(
+            [(ig_h, ig), (vi_h, vi), (fl_h, fl), (w_h.at[:, pl.ds(pl.multiple_of(odd * side, side), side)], wall.at[me, 0]), (ft_h, ft), (it_h, it), (og_h, og), (sk_h, sk),
+             (w_h.at[:, pl.ds(pl.multiple_of((1 - odd) * side, side), side)], wl)]
+        )
+    ]
+    for copy in loads:
+        copy.start()
 
     sent = []
     kinds = {}
@@ -197,12 +197,12 @@
         w_send(h, stage, ra, "FL")
 
     relay(1, 0, 0)
-    relay(0, 1, 0)
     relay(0, 0, 0)
     for ra in (-1, 1):
         for what in ("R", "L"):
             for h in (0, 1):
                 w_send(h, 1, ra, what)
+    relay(0, 1, 0)
 
     loads[6].wait()
     loads[7].wait()
@@ -220,9 +220,8 @@
         return there, there // 2 == core, lax.rem(there, 2)
 
     def swap(n, k):
-        two = pl.ds(k, 2)
         return pltpu.make_async_remote_copy(
-            src_ref=other.at[n, two], dst_ref=cr.at[n, two],
+            src_ref=other.at[n, k], dst_ref=cr.at[n, k],
             send_sem=osem_s.at[n * RING + k], recv_sem=osem_r.at[n * RING + k],
             device_id={"ch": ch_of(0, 1 - core)},
         )
@@ -249,13 +248,11 @@
                     part[near_n, k + i] = value[:, i * side : (i + 1) * side]
                 else:
                     other[near_n, k + i] = value[:, i * side : (i + 1) * side].astype(BF16)
-            if not mine:
-                swap(near_n, k).start()
+                    swap(near_n, k + i).start()
 
     def pass_on(n):
         for k in range(RING - 1):
-            if k % 2 == 0:
-                swap(n, k).wait_recv()
+            swap(n, k).wait_recv()
             xs[n, k] = (part[n, k] + cr[n, k].astype(F32)).astype(BF16)
             share(n, k).start()
 
@@ -277,7 +274,7 @@
             def _():
                 for i in (0, 1):
                     other[n, k + i] = value[:, i * side : (i + 1) * side].astype(BF16)
-                swap(n, k).start()
+                    swap(n, k + i).start()
 
     def spread(ry):
         there, mine, n = group_of(ry)
@@ -287,6 +284,7 @@
             pass_on(n)
 
     def collect(n):
+        swap(n, RING - 1).wait_recv()
         total = part[n, RING - 1] + cr[n, RING - 1].astype(F32)
         for k in range(RING - 1):
             share(n, k).wait_recv()
@@ -309,7 +307,7 @@
 
         @pl.when(jnp.logical_not(mine))
         def _():
-            for k in (0, 2):
+            for k in range(RING):
                 swap(n, k).wait_send()
 
     for what in ("FR", "FL"):
@@ -342,37 +340,15 @@
     exchanged(csend, cx, 2).wait_send()
     for copy in sent:
         copy.wait_send()
-    there, mine, n = group_of(2)
-
-    def last_term(h, k):
-        two = [wall[lax.rem(x + turns[k + i] + RING, RING) * RING + there, h] for i in (0, 1)]
-        return jnp.dot(mixes[h], jnp.concatenate(two, axis=1), preferred_element_type=F32)
-
     for what in ("FR", "FL"):
         w_wait(0, 1, 2, what)
-    early[0] = last_term(0, 0)
-    early[1] = last_term(0, 2)
-    for what in ("FR", "FL"):
         for ra in (0, -1, 1, 2):
             w_wait(1, 1, ra, what)
-    for k in (0, 2):
-        value = early[k // 2] + last_term(1, k)
-
-        @pl.when(mine)
-        def _():
-            for i in (0, 1):
-                part[n, k + i] = value[:, i * side : (i + 1) * side]
-
-        @pl.when(jnp.logical_not(mine))
-        def _():
-            for i in (0, 1):
-                other[n, k + i] = value[:, i * side : (i + 1) * side].astype(BF16)
-            swap(n, k).start()
-
+    multiply(2)
     spread(2)
     finish(0)
     collect(near_n)
-    for k in (0, 2):
+    for k in range(RING):
         swap(near_n, k).wait_send()
     for k in range(RING - 1):
         share(near_n, k).wait_send()
@@ -417,7 +393,6 @@
         pltpu.VMEM((2, RING, rows, cols // 2), BF16),
         pltpu.VMEM((2, RING, rows, cols // 2), BF16),
         pltpu.VMEM((2, RING, rows, cols // 2), BF16),
-        pltpu.VMEM((2, rows, cols), F32),
         dma((9,)),
         dma((3,)), dma((3,)),
         dma((1,)), dma((40,)),

time: 49.1 us -> 49 us (level)
  no operation moved by 1% of the time
where the time goes in v7:
time: 49 us; the launch traced here: 48.9 us
  Pallas kernels  48.2 us (98%)
  local copies, waits for them, and re-layouts  0.71 us (1%)
    pallas_call x1, Pallas kernels, per_device(): pl.pallas_call(kernel, out_shape=jax.ShapeDtypeStruct((rows, chans), BF16...  48.2 us

profile of v7, /device:TPU:1, one launch (start us, length us, event | category | flops | bytes accessed | tf_op | source)
XLA Modules:
  0.0 48.9 jit_solution(6467427207012057575)
XLA Ops:
  0.0 48.2 %long_conv_layer.1 = bf16[256,512]{1,0:T(8,128)(2,1)S(1)} custom-call(bf16[256,512]{1,0:T(8,128)(2,1)} %og_h.1, bf16[256,512]{1,0:T(8,128)(2,1)} %ig_h.1, bf16[256,512]{1,0:T(8,128)(2,1)} %vi_h.1, f32[256,512]{1,0:T(8,128)} %fl_h.1, f32[1,512]{1,0:T(1,128)} %bitcast.1, bf16[512,256]{1,0:T(8,128)(2,1)} %w_h.1, bf16[256,512]{1,0:T(8,128)(2,1)} %constant.4.clone.ft_h, ...), custom_call_target="tpu_custom_call" | custom-call | tf_op jit(solution)/shard_map/long_conv_layer/pallas_call | solution.py:407
  48.2 0.7 %copy.10 = bf16[256,512]{1,0:T(8,128)(2,1)} copy(bf16[256,512]{1,0:T(8,128)(2,1)S(1)} %long_conv_layer.1) | data formatting | bytes 524288

commit v8 on v6

--- a/solution.py
+++ b/solution.py
@@ -220,9 +220,8 @@
         return there, there // 2 == core, lax.rem(there, 2)
 
     def swap(n, k):
-        two = pl.ds(k, 2)
         return pltpu.make_async_remote_copy(
-            src_ref=other.at[n, two], dst_ref=cr.at[n, two],
+            src_ref=other.at[n, k], dst_ref=cr.at[n, k],
             send_sem=osem_s.at[n * RING + k], recv_sem=osem_r.at[n * RING + k],
             device_id={"ch": ch_of(0, 1 - core)},
         )
@@ -249,13 +248,11 @@
                     part[near_n, k + i] = value[:, i * side : (i + 1) * side]
                 else:
                     other[near_n, k + i] = value[:, i * side : (i + 1) * side].astype(BF16)
-            if not mine:
-                swap(near_n, k).start()
+                    swap(near_n, k + i).start()
 
     def pass_on(n):
         for k in range(RING - 1):
-            if k % 2 == 0:
-                swap(n, k).wait_recv()
+            swap(n, k).wait_recv()
             xs[n, k] = (part[n, k] + cr[n, k].astype(F32)).astype(BF16)
             share(n, k).start()
 
@@ -277,7 +274,7 @@
             def _():
                 for i in (0, 1):
                     other[n, k + i] = value[:, i * side : (i + 1) * side].astype(BF16)
-                swap(n, k).start()
+                    swap(n, k + i).start()
 
     def spread(ry):
         there, mine, n = group_of(ry)
@@ -287,6 +284,7 @@
             pass_on(n)
 
     def collect(n):
+        swap(n, RING - 1).wait_recv()
         total = part[n, RING - 1] + cr[n, RING - 1].astype(F32)
         for k in range(RING - 1):
             share(n, k).wait_recv()
@@ -309,7 +307,7 @@
 
         @pl.when(jnp.logical_not(mine))
         def _():
-            for k in (0, 2):
+            for k in range(RING):
                 swap(n, k).wait_send()
 
     for what in ("FR", "FL"):
@@ -367,12 +365,12 @@
         def _():
             for i in (0, 1):
                 other[n, k + i] = value[:, i * side : (i + 1) * side].astype(BF16)
-            swap(n, k).start()
+                swap(n, k + i).start()
 
     spread(2)
     finish(0)
     collect(near_n)
-    for k in (0, 2):
+    for k in range(RING):
         swap(near_n, k).wait_send()
     for k in range(RING - 1):
         share(near_n, k).wait_send()

time: 49.1 us -> 49.1 us (level)
  no operation moved by 1% of the time
where the time goes in v8:
time: 49.1 us; the launch traced here: 48.9 us
  Pallas kernels  48.2 us (98%)
  local copies, waits for them, and re-layouts  0.71 us (1%)
    pallas_call x1, Pallas kernels, per_device(): pl.pallas_call(kernel, out_shape=jax.ShapeDtypeStruct((rows, chans), BF16...  48.2 us

profile of v8, /device:TPU:1, one launch (start us, length us, event | category | flops | bytes accessed | tf_op | source)
XLA Modules:
  0.0 48.9 jit_solution(9535178005186420070)
XLA Ops:
  0.0 48.2 %long_conv_layer.1 = bf16[256,512]{1,0:T(8,128)(2,1)S(1)} custom-call(bf16[256,512]{1,0:T(8,128)(2,1)} %og_h.1, bf16[256,512]{1,0:T(8,128)(2,1)} %ig_h.1, bf16[256,512]{1,0:T(8,128)(2,1)} %vi_h.1, f32[256,512]{1,0:T(8,128)} %fl_h.1, f32[1,512]{1,0:T(1,128)} %bitcast.1, bf16[512,256]{1,0:T(8,128)(2,1)} %w_h.1, bf16[256,512]{1,0:T(8,128)(2,1)} %constant.4.clone.ft_h, ...), custom_call_target="tpu_custom_call" | custom-call | tf_op jit(solution)/shard_map/long_conv_layer/pallas_call | solution.py:430
  48.2 0.7 %copy.10 = bf16[256,512]{1,0:T(8,128)(2,1)} copy(bf16[256,512]{1,0:T(8,128)(2,1)S(1)} %long_conv_layer.1) | data formatting | bytes 524288
